TPU v7x, 256 devices: a whole 4x4x8 slice. The times are simulated.
256 devices in a mesh: seq: 64 (over z, y, core), fsdp: 4 (over x).
Axes of the slice: x: 4, y: 4, z: 8, core: 2. Of those that a mesh axis runs over, the one named last changes fastest.
Arguments:
- inputs: bfloat16 [4, 8192, 3584], P('fsdp', 'seq'), may hold values from -36 to 36
- keys_queries: bfloat16 [4, 8192, 256], P('fsdp', 'seq'), may hold values from -0.29882812 to 0.29882812
- log_decay: float32 [4, 56, 8192], P('fsdp', None, 'seq'), may hold values from -1.5 to 0, as said below
- skip: float32 [56], replicated, may hold values from 0.5 to 1.5
- classifier: bfloat16 [3584, 128], P('fsdp'), may hold values from -0.09375 to 0.09375
Outputs:
- mixed: bfloat16 [4, 8192, 3584], P('fsdp', 'seq')
- logits: float32 [4, 128], P('fsdp')
Inputs may be any that keep to these rules, and one draw needn't show every extreme that they name: `log_decay`: log-decays are negative.
All inputs are finite; a program needn't handle non-finite values.
Results may differ from a plain program's by a relative error of at most 0.0051.
Values may be sent and summed in bfloat16 or wider, within the bound.
A program may use at most 256 MiB of HBM per device.

v0:
```python
import jax
import jax.numpy as jnp
from jax import lax
from jax.sharding import PartitionSpec as P

N = 128
GROUP = 128


epsilon = 1e-06


def linker(earlier, latter):
    return (earlier[0] + latter[0], jnp.exp(latter[0]) * earlier[1] + latter[1])


def local(inputs, keys_queries, log_decay, skip, classifier):
    copies, positions, channels = inputs.shape
    head_count = log_decay.shape[1]
    head_dim = channels // head_count
    blocks = positions // GROUP
    key_rows = keys_queries[:, :, :N].reshape(copies, blocks, GROUP, N)
    queries = keys_queries[:, :, N:].reshape(copies, blocks, GROUP, N)
    values = inputs.reshape(copies, blocks, GROUP, head_count, head_dim)
    cumulative = jnp.cumsum(log_decay.reshape(copies, head_count, blocks, GROUP), axis=-1)
    block_decay = cumulative[..., -1]
    weighted = (key_rows[:, None] * jnp.exp(block_decay[..., None] - cumulative)[..., None]).astype(
        jnp.bfloat16
    )
    block_state = jnp.einsum(
        "chkun,ckuhp->kchnp", weighted, values, preferred_element_type=jnp.float32
    )

    def advance(running, member):
        return (jnp.exp(member[0])[..., None, None] * running + member[1], running)

    device_state, starts = lax.scan(
        advance, jnp.zeros_like(block_state[0]), (jnp.moveaxis(block_decay, 2, 0), block_state)
    )
    device_decay = jnp.sum(block_decay, axis=-1)
    axis_count = lax.axis_size("seq")
    flattened = device_state.reshape(copies, head_count, 1, N * head_dim)
    decay_copies = jnp.broadcast_to(
        device_decay[:, :, None, None], (copies, head_count, 1, axis_count)
    )
    totals = lax.associative_scan(
        linker,
        (
            lax.all_to_all(decay_copies, "seq", split_axis=3, concat_axis=2, tiled=True),
            lax.all_to_all(flattened, "seq", split_axis=3, concat_axis=2, tiled=True),
        ),
        axis=2,
    )[1]
    shifted = jnp.concatenate([jnp.zeros_like(totals[:, :, :1]), totals[:, :, :-1]], axis=2)
    incoming = lax.all_to_all(shifted, "seq", split_axis=2, concat_axis=3, tiled=True)
    incoming = incoming.reshape(copies, head_count, N, head_dim)
    preceding = jnp.moveaxis(jnp.cumsum(block_decay, axis=-1) - block_decay, 2, 0)
    carried = (jnp.exp(preceding)[..., None, None] * incoming[None] + starts).astype(jnp.bfloat16)
    growth = jnp.exp(cumulative).transpose(0, 2, 3, 1)[..., None]
    carried_out = (
        jnp.einsum("ckqn,kchnp->ckqhp", queries, carried, preferred_element_type=jnp.float32)
        * growth
    )
    causal = jnp.arange(GROUP)[:, None] >= jnp.arange(GROUP)[None, :]
    scores = jnp.einsum("cktn,ckun->cktu", queries, key_rows, preferred_element_type=jnp.float32)
    decay_gap = jnp.where(causal, cumulative[..., :, None] - cumulative[..., None, :], -jnp.inf)
    mixing = (scores[:, None] * jnp.exp(decay_gap)).astype(jnp.bfloat16)
    diagonal = jnp.einsum("chktu,ckuhp->ckthp", mixing, values, preferred_element_type=jnp.float32)
    mixed_full = diagonal + carried_out + skip[:, None] * values.astype(jnp.float32)
    mixed = mixed_full.astype(jnp.bfloat16).reshape(copies, positions, channels)
    partial_sum = jnp.sum(mixed_full, axis=(1, 2)).reshape(copies, channels)
    pooled = lax.psum(partial_sum, "seq") / (positions * lax.axis_size("seq"))
    normed = (
        pooled / jnp.sqrt(jnp.mean(pooled * pooled, axis=-1, keepdims=True) + epsilon)
    ).astype(jnp.bfloat16)
    logits = jnp.dot(
        normed,
        lax.all_gather(classifier, "fsdp", axis=0, tiled=True),
        preferred_element_type=jnp.float32,
    )
    return (mixed, logits)


def solution(mesh):
    return jax.shard_map(
        local,
        mesh=mesh,
        in_specs=(
            P("fsdp", "seq", None),
            P("fsdp", "seq", None),
            P("fsdp", None, "seq"),
            P(),
            P("fsdp", None),
        ),
        out_specs=(P("fsdp", "seq", None), P("fsdp", None)),
        check_vma=False,
    )
```

profile of v0, /device:TPU:2, one launch (start us, length us, event | category | flops | bytes accessed | tf_op | source)
XLA Modules:
  0.0 497.6 jit_solution(18033312582586399048)
XLA Ops:
  0.6 1.1 reduce_window_sum.17
  1.7 0.2 multiply_reduce_fusion
  1.9 0.6 broadcast_in_dim.18
  2.5 12.1 %all-to-all-start.1 = ((f32[1,56,1,64]{1,2,0,3:T(1,128)}), f32[1,56,1,64]{1,2,0,3:T(1,128)S(1)}, u32[]{:S(2)}, u32[]{:S(2)}) async-start(f32[1,56,1,64]{1,2,0,3:T(1,128)} %broadcast_in_dim.18), calls=%async_computation.1 | async-start | bytes 65536 | tf_op jit(solution)/shard_map/all_to_all | solution.py:49
  14.7 1.6 copy.45
  16.3 1.3 fusion.10
  17.6 4.5 copy.57
  22.1 0.5 broadcast.116
  22.6 38.4 %reduce.6 = f32[8192,56]{1,0:T(8,128)} reduce(f32[8192,1,1,56]{3,2,1,0:T(1,128)} %bitcast.76, f32[]{:T(128)} %broadcast.116), dimensions={1,2}, to_apply=%bitcast.65.reduce_sub_computation | reduce | bytes 3670020
  61.0 6.9 %reshape.245 = f32[64,1,7168]{2,1,0:T(1,128)} reshape(f32[8192,56]{1,0:T(8,128)} %reduce.6) | data formatting | bytes 3670016
  67.9 10.5 %all-to-all-start = ((f32[64,1,7168]{2,1,0:T(1,128)}), f32[64,1,7168]{2,1,0:T(1,128)S(1)}, u32[]{:S(2)}, u32[]{:S(2)}) async-start(f32[64,1,7168]{2,1,0:T(1,128)} %reshape.245), calls=%async_computation | async-start | bytes 3670016 | tf_op jit(solution)/shard_map/all_to_all | solution.py:50
  78.8 45.2 %all-to-all-done = f32[64,1,7168]{2,1,0:T(1,128)S(1)} async-done(((f32[64,1,7168]{2,1,0:T(1,128)}), f32[64,1,7168]{2,1,0:T(1,128)S(1)}, u32[]{:S(2)}, u32[]{:S(2)}) %all-to-all-start) | async-done | bytes 1835040 | tf_op jit(solution)/shard_map/all_to_all | solution.py:50
  124.0 6.8 %reduce.7 = f32[64,7168]{1,0:T(8,128)} reduce(f32[64,1,7168]{2,1,0:T(1,128)S(1)} %all-to-all-done, f32[]{:T(128)} %broadcast.116), dimensions={1}, to_apply=%all_to_all.10.reduce_sub_computation | reduce | bytes 3670020 | tf_op jit(solution)/shard_map/all_to_all | solution.py:50
  130.7 11.1 %reshape.246 = f32[8192,1,1,56]{3,2,1,0:T(1,128)} reshape(f32[64,7168]{1,0:T(8,128)} %reduce.7) | data formatting | bytes 3670016
  141.8 4.1 fusion.34
  145.9 1.5 slice.192
  147.4 0.6 slice.195
  148.0 2.2 copy.60
  150.2 1.5 copy.61
  151.7 1.5 multiply_add_fusion
  153.2 0.2 slice_add_fusion
  153.4 0.1 slice_add_fusion.1
  154.3 0.1 fusion.13
  154.6 0.2 fusion.12
  154.9 0.2 pad.46
  155.0 0.4 pad.47
  155.5 0.9 copy-done.2
  156.4 1.0 add.138
  157.4 16.4 %pad.85 = f32[1,56,64,128]{3,1,0,2:T(8,128)} pad(f32[1,56,32,128]{3,1,0,2:T(8,128)} %add.138, f32[]{:T(128)} %constant.16.clone.1), padding=0_0_0x0_0_0x1_0_1x0_0_0 | pad | bytes 2752516
  173.8 1.5 copy.62
  175.4 1.8 fusion.11
  177.2 11.0 %pad.61 = f32[1,56,63,128]{3,1,0,2:T(8,128)} pad(f32[1,56,32,128]{3,1,0,2:T(8,128)S(1)} %pad_maximum_fusion, f32[]{:T(128)} %constant.16.clone.1), padding=0_0_0x0_0_0x0_0_1x0_0_0 | pad | bytes 2723844 | tf_op jit(solution)/shard_map/slice | solution.py:54
  188.3 1.7 slice_add_fusion.5
  190.0 1.3 concatenate.23
  191.3 5.3 %all-to-all-start.2 = ((f32[1,56,64,128]{3,1,0,2:T(8,128)}), f32[1,56,64,128]{3,1,0,2:T(8,128)S(1)}, u32[]{:S(2)}, u32[]{:S(2)}) async-start(f32[1,56,64,128]{3,1,0,2:T(8,128)} %concatenate.23), calls=%async_computation.2 | async-start | bytes 3670016 | tf_op jit(solution)/shard_map/all_to_all | solution.py:55
  196.6 2.6 copy.54
  199.3 0.1 fusion.16
  199.4 2.6 fusion
  202.0 15.5 %all_gather.3 = bf16[3584,128]{1,0:T(8,128)(2,1)} all-gather(bf16[896,128]{1,0:T(8,128)(2,1)S(1)} %copy-done.10), channel_id=1, replica_groups=mesh['seq'=64,'fsdp'=4] {'fsdp'}, dimensions={0}, use_global_device_ids=true | all-gather | bytes 1146880 | tf_op jit(solution)/shard_map/all_gather | solution.py:78
  217.5 24.9 %all-to-all-done.2 = f32[1,56,64,128]{3,1,0,2:T(8,128)S(1)} async-done(((f32[1,56,64,128]{3,1,0,2:T(8,128)}), f32[1,56,64,128]{3,1,0,2:T(8,128)S(1)}, u32[]{:S(2)}, u32[]{:S(2)}) %all-to-all-start.2) | async-done | bytes 1835040 | tf_op jit(solution)/shard_map/all_to_all | solution.py:55
  242.4 0.2 multiply_convert_fusion.4
  242.6 0.2 copy.52
  242.8 1.7 convert_element_type.57
  244.6 3.3 fusion.35
  248.0 246.3 %psum.7 = f32[1,3584]{1,0:T(1,128)S(1)} all-reduce(f32[1,3584]{1,0:T(1,128)S(1)} %reshape.236), channel_id=1, replica_groups=mesh['seq'=64,'fsdp'=4] {'seq'}, use_global_device_ids=true, to_apply=%region_2.3 | all-reduce | flops 3584 | bytes 28672 | tf_op jit(solution)/shard_map/psum | solution.py:72
  494.3 0.6 multiply_reduce_fusion.1
  495.6 1.3 copy.55
  496.9 0.7 fusion.25
  (79 shorter events, 1.6 us)
Async XLA Ops:
  0.6 15.7 %copy-start.8 = (bf16[1,128,256]{2,1,0:T(8,128)(2,1)S(1)}, bf16[1,128,256]{2,1,0:T(8,128)(2,1)}, u32[]{:S(2)}) copy-start(bf16[1,128,256]{2,1,0:T(8,128)(2,1)} %param.6) | copy-start | bytes 196612
  2.5 65.4 %all-to-all-start.1 = ((f32[1,56,1,64]{1,2,0,3:T(1,128)}), f32[1,56,1,64]{1,2,0,3:T(1,128)S(1)}, u32[]{:S(2)}, u32[]{:S(2)}) async-start(f32[1,56,1,64]{1,2,0,3:T(1,128)} %broadcast_in_dim.18), calls=%async_computation.1 | async-start | bytes 65536 | tf_op jit(solution)/shard_map/all_to_all | solution.py:49
  16.3 5.8 %copy-start.5 = (bf16[1,128,3584]{1,2,0:T(8,128)(2,1)}, bf16[1,128,3584]{1,2,0:T(8,128)(2,1)S(1)}, u32[]{:S(2)}) copy-start(bf16[1,128,3584]{1,2,0:T(8,128)(2,1)S(1)} %copy.45) | copy-start | bytes 2752516
  67.9 56.0 %all-to-all-start = ((f32[64,1,7168]{2,1,0:T(1,128)}), f32[64,1,7168]{2,1,0:T(1,128)S(1)}, u32[]{:S(2)}, u32[]{:S(2)}) async-start(f32[64,1,7168]{2,1,0:T(1,128)} %reshape.245), calls=%async_computation | async-start | bytes 3670016 | tf_op jit(solution)/shard_map/all_to_all | solution.py:50
  141.8 4.1 copy-start
  155.4 0.9 copy-start.2
  157.4 16.4 %copy-start.1 = (f32[1,56,31,128]{1,3,2,0:T(8,128)S(1)}, f32[1,56,31,128]{1,3,2,0:T(8,128)}, u32[]{:S(2)}) copy-start(f32[1,56,31,128]{1,3,2,0:T(8,128)} %slice.192) | copy-start | bytes 2666500
  173.8 1.5 copy-start.9
  177.2 11.1 %copy-start.4 = (f32[1,56,64,128]{3,1,0,2:T(8,128)S(1)}, f32[1,56,64,128]{3,1,0,2:T(8,128)}, u32[]{:S(2)}) copy-start(f32[1,56,64,128]{3,1,0,2:T(8,128)} %pad.85) | copy-start | bytes 5505028
  191.3 51.1 %all-to-all-start.2 = ((f32[1,56,64,128]{3,1,0,2:T(8,128)}), f32[1,56,64,128]{3,1,0,2:T(8,128)S(1)}, u32[]{:S(2)}, u32[]{:S(2)}) async-start(f32[1,56,64,128]{3,1,0,2:T(8,128)} %concatenate.23), calls=%async_computation.2 | async-start | bytes 3670016 | tf_op jit(solution)/shard_map/all_to_all | solution.py:55
  196.6 2.8 copy-start.6
  199.4 2.6 copy-start.10
  242.8 1.8 copy-start.3
  242.8 1.8 copy-start.11
  247.9 249.0 %copy-start.7 = (bf16[3584,128]{1,0:T(8,128)(2,1)S(1)}, bf16[3584,128]{1,0:T(8,128)(2,1)}, u32[]{:S(2)}) copy-start(bf16[3584,128]{1,0:T(8,128)(2,1)} %all_gather.3) | copy-start | bytes 2752516
where the time goes:
time: 500 us; the launch traced here: 498 us
  blocking collectives  262 us (52%)
  local copies, waits for them, and re-layouts  73.5 us (15%)
  waiting for transfers between devices  70.1 us (14%)
  other arithmetic  54.6 us (11%)
  starting transfers between devices  27.9 us (6%)
  matrix products  7.99 us (2%)
    psum x1, blocking collectives, local(): pooled = lax.psum(partial_sum, 'seq') / (positions * lax.axis_size('seq'))  246 us
    all_to_all x1, waiting for transfers between devices, local(): lax.all_to_all(flattened, 'seq', split_axis=3, concat_axis=2, tiled=True)  45.2 us
    unnamed x34, local copies, waits for them, and re-layouts  44 us
    unnamed x1, other arithmetic  38.4 us
    all_to_all x1, waiting for transfers between devices, local(): lax.all_to_all(shifted, 'seq', split_axis=2, concat_axis=3, tiled=True)  24.9 us
    all_gather x1, blocking collectives, local(): lax.all_gather(classifier, 'fsdp', axis=0, tiled=True)  15.5 us
    all_to_all x1, starting transfers between devices, local(): lax.all_to_all(decay_copies, 'seq', split_axis=3, concat_axis=2, tiled=True)  12.1 us
    slice x1, local copies, waits for them, and re-layouts, local(): totals[:, :, :-1]  11 us
  transfers between devices with their start and end apart: 3, of which 2 were waited for; matrix products, arithmetic and copies ran while one was open for 12% of the time, Pallas kernels for 0%

commit v1 on v0

v1 whole, which is shorter than its diff:
```python
import jax
import jax.numpy as jnp
from jax import lax
from jax.experimental import pallas as pl
from jax.experimental.pallas import tpu as pltpu
from jax.sharding import PartitionSpec as P

MESH = pl.DeviceIdType.MESH
F32, BF16 = jnp.float32, jnp.bfloat16

N = 128
G = 128
L = 128
NZ, NY, NC, NX = 8, 4, 2, 4
TILES = 28
M = TILES // NY
ROWS = M * 8
EPS = 1e-06


def spread(x):
    return jnp.concatenate(
        [jnp.broadcast_to(x[m : m + 1, :], (8, L)) for m in range(M)], axis=0
    )


def kernel(
    v_ref, kq_ref, ld_ref, skip_ref, cls_ref, mixed_ref, logits_ref,
    grow, local_out, own_state, pair_recv, pair_total, plane_recv, plane_prefix,
    axis_send, axis_recv, axis_prefix, start_plane, start_send, start_chip,
    carried, carried_send, table,
    decay_own, decay_pair, decay_chip, decay_plane, decay_sum, decay_axis, factor, factor_chip,
    pool_own, pool_pair, pool_pair_sum, pool_plane, pool_plane_sum, pool_axis,
    pair_s, pair_r, plane_s, plane_r, axis_s, axis_r, table_s, table_r, local_sem,
):
    me, x = lax.axis_index("seq"), lax.axis_index("fsdp")
    c = lax.rem(me, NC)
    y = lax.rem(me // NC, NY)
    z = me // (NC * NY)
    other = 1 - c
    partner = me + 1 - 2 * c
    ys = [lax.rem(y + k, NY) for k in range(NY)]
    zs = [lax.rem(z + k, NZ) for k in range(NZ)]

    def at(z_, y_, c_):
        return (z_ * NY + y_) * NC + c_

    to_y = [at(z, ys[k], c) for k in range(NY)]
    to_z = [at(zs[k], y, c) for k in range(NZ)]

    barrier = pltpu.get_barrier_semaphore()

    def greet(who):
        pl.semaphore_signal(barrier, inc=1, device_id=who, device_id_type=MESH)

    greet({"seq": partner})
    for k in range(1, NY):
        greet({"seq": to_y[k]})
    for k in range(1, NZ):
        greet({"seq": to_z[k]})
    for k in range(1, NX):
        greet({"fsdp": lax.rem(x + k, NX)})

    sends = []

    def push(src, dst, send, recv, who):
        copy = pltpu.make_async_remote_copy(
            src_ref=src, dst_ref=dst, send_sem=send, recv_sem=recv,
            device_id=who, device_id_type=MESH,
        )
        copy.start()
        sends.append(copy)
        return copy

    left_half = lax.broadcasted_iota(jnp.int32, (1, L), 1) < 64
    for g in range(NY):
        even = jnp.sum(ld_ref[pl.ds(2 * M * g, M, stride=2), :], axis=1, keepdims=True)
        odd = jnp.sum(ld_ref[pl.ds(2 * M * g + 1, M, stride=2), :], axis=1, keepdims=True)
        decay_own[g, 0:M, :] = jnp.where(left_half, even, odd)
        decay_own[g, M:8, :] = jnp.zeros((8 - M, L), F32)

    row = lax.broadcasted_iota(jnp.int32, (G, G), 0)
    col = lax.broadcasted_iota(jnp.int32, (G, G), 1)
    causal = row >= col
    lower = jnp.where(causal, 1.0, 0.0).astype(F32)
    log_decay = ld_ref[...]
    cum = lax.dot_general(
        log_decay, lower, (((1,), (1,)), ((), ())),
        precision=lax.Precision.HIGHEST, preferred_element_type=F32,
    )
    cum_t = lax.dot_general(
        lower, log_decay, (((1,), (1,)), ((), ())),
        precision=lax.Precision.HIGHEST, preferred_element_type=F32,
    )
    keys = kq_ref[:, :N]
    queries = kq_ref[:, N:]
    keys_t = keys.T

    pl.semaphore_wait(barrier, 1 + (NY - 1) + (NZ - 1) + (NX - 1))

    table_copies = [
        push(cls_ref, table.at[x], table_s.at[k], table_r.at[k], {"fsdp": lax.rem(x + k, NX)})
        for k in range(1, NX)
    ]
    own_rows = pltpu.make_async_copy(cls_ref, table.at[x], local_sem)
    own_rows.start()

    pair_decay = push(decay_own, decay_pair, pair_s.at[4], pair_r.at[4], {"seq": partner})
    pair_copies = []
    for g in range(NY):
        for m in range(M):
            j = g * M + m
            lanes = slice(j * L, (j + 1) * L)
            level = jnp.where(left_half, cum_t[:, 2 * j : 2 * j + 1], cum_t[:, 2 * j + 1 : 2 * j + 2])
            grow[j] = level
            weight = jnp.exp(level[G - 1 : G, :] - level)
            weighted = (v_ref[:, lanes].astype(F32) * weight).astype(BF16)
            state = jnp.dot(keys_t, weighted, preferred_element_type=F32).astype(BF16)
            for half in range(NC):
                for b in range(NZ):
                    first = half * 64 + b * 8
                    own_state[half, g, b, m * 8 : m * 8 + 8, :] = state[first : first + 8, :]
        pair_copies.append(
            push(own_state.at[other, g], pair_recv.at[g], pair_s.at[g], pair_r.at[g], {"seq": partner})
        )

    def inside(g):
        scores = lax.dot_general(
            queries, keys, (((1,), (1,)), ((), ())), preferred_element_type=F32
        )
        scores = jnp.where(causal, scores, 0.0)
        for m in range(M):
            j = g * M + m
            lanes = slice(j * L, (j + 1) * L)
            parts = []
            for h in (2 * j, 2 * j + 1):
                gap = jnp.minimum(cum_t[:, h : h + 1] - cum[h : h + 1, :], 0.0)
                parts.append((scores * jnp.exp(gap)).astype(BF16))
            value = v_ref[:, lanes]
            zero = jnp.zeros_like(value)
            stacked = jnp.concatenate(
                [jnp.where(left_half, value, zero), jnp.where(left_half, zero, value)], axis=0
            )
            diagonal = jnp.dot(
                jnp.concatenate(parts, axis=1), stacked, preferred_element_type=F32
            )
            direct = jnp.where(left_half, skip_ref[2 * j], skip_ref[2 * j + 1])
            local_out[j] = diagonal + direct * value.astype(F32)
            grow[j] = jnp.exp(grow[j])

    inside(0)

    pair_decay.wait_recv()
    for g in range(NY):
        mine, theirs = decay_own[g], decay_pair[g]
        decay_chip[g] = mine + theirs
        factor[0, g] = spread(jnp.where(c == 0, jnp.exp(theirs), 1.0))
        factor[1, g] = spread(jnp.where(c == 0, 1.0, jnp.exp(mine)))
        factor_chip[g] = spread(jnp.exp(jnp.where(c == 0, mine, theirs)))
    for copy in pair_copies:
        copy.wait_recv()

    plane_copies = []
    for k in (2, 1, 3, 0):
        g = ys[k]

        @pl.loop(0, NZ)
        def _(b, g=g, k=k):
            total = factor[0, g] * own_state[c, g, b].astype(F32) + factor[1, g] * pair_recv[g, b].astype(F32)
            if k == 0:
                plane_recv[y, b] = total.astype(BF16)
            else:
                pair_total[k, b] = total.astype(BF16)

        if k == 0:
            decay_plane[y] = decay_chip[y]
        else:
            plane_copies.append(
                push(decay_chip.at[g], decay_plane.at[y], plane_s.at[3 + k], plane_r.at[3 + k], {"seq": to_y[k]})
            )
            plane_copies.append(
                push(pair_total.at[k], plane_recv.at[y], plane_s.at[k], plane_r.at[k], {"seq": to_y[k]})
            )

    for g in range(1, NY):
        inside(g)
    for copy in plane_copies:
        copy.wait_recv()

    run = jnp.zeros((8, L), F32)
    for k in range(NY):
        factor[2, k] = spread(jnp.exp(decay_plane[k]))
        factor[3, k] = spread(jnp.exp(run))
        run = run + decay_plane[k]
    decay_sum[...] = run
    decay_axis[z] = run

    axis_copies = []
    for k in (4, 5, 3, 6, 2, 7, 1, 0):
        b = zs[k]
        total = jnp.zeros((ROWS, L), F32)
        for q in range(NY):
            plane_prefix[q, b] = total
            total = factor[2, q] * total + plane_recv[q, b].astype(F32)
        if k == 0:
            axis_recv[z] = total.astype(BF16)
        else:
            axis_send[k] = total.astype(BF16)
            axis_copies.append(
                push(decay_sum, decay_axis.at[z], axis_s.at[8 + k], axis_r.at[8 + k], {"seq": to_z[k]})
            )
            axis_copies.append(
                push(axis_send.at[k], axis_recv.at[z], axis_s.at[k], axis_r.at[k], {"seq": to_z[k]})
            )
    for copy in axis_copies:
        copy.wait_recv()

    total = jnp.zeros((ROWS, L), F32)
    for q in range(NZ):
        axis_prefix[q] = total.astype(BF16)
        if q < NZ - 1:
            total = spread(jnp.exp(decay_axis[q])) * total + axis_recv[q].astype(F32)
    back_copies = [
        push(axis_prefix.at[zs[k]], start_plane.at[z], axis_s.at[16 + k], axis_r.at[16 + k], {"seq": to_z[k]})
        for k in (4, 5, 3, 6, 2, 7, 1)
    ]
    start_plane[z] = axis_prefix[z]
    for copy in back_copies:
        copy.wait_recv()

    chip_copies = []
    for k in (2, 1, 3, 0):
        g = ys[k]

        @pl.loop(0, NZ)
        def _(b, g=g, k=k):
            start = factor[3, g] * start_plane[b].astype(F32) + plane_prefix[g, b]
            if k == 0:
                start_chip[y, b] = start.astype(BF16)
            else:
                start_send[k, b] = start.astype(BF16)

        if k:
            chip_copies.append(
                push(start_send.at[k], start_chip.at[y], plane_s.at[6 + k], plane_r.at[6 + k], {"seq": to_y[k]})
            )
    for copy in chip_copies:
        copy.wait_recv()

    half_copies = []
    for g in range(NY):

        @pl.loop(0, NZ)
        def _(b, g=g):
            first = start_chip[g, b].astype(F32)
            state = jnp.where(c == 0, own_state[c, g, b].astype(F32), pair_recv[g, b].astype(F32))
            second = factor_chip[g] * first + state
            carried[c, g, b] = jnp.where(c == 0, first, second).astype(BF16)
            carried_send[g, b] = jnp.where(c == 0, second, first).astype(BF16)

        half_copies.append(
            push(carried_send.at[g], carried.at[c, g], pair_s.at[5 + g], pair_r.at[5 + g], {"seq": partner})
        )

    pool_own[...] = jnp.zeros_like(pool_own)
    for g in range(NY):
        half_copies[g].wait_recv()
        for m in range(M):
            j = g * M + m
            start = jnp.concatenate(
                [
                    carried[half, g, b, m * 8 : m * 8 + 8, :]
                    for half in range(NC)
                    for b in range(NZ)
                ],
                axis=0,
            )
            full = local_out[j] + grow[j] * jnp.dot(queries, start, preferred_element_type=F32)
            mixed_ref[:, j * L : (j + 1) * L] = full.astype(BF16)
            pool_own[j : j + 1, :] = jnp.sum(full, axis=0, keepdims=True)

    pool_pair[c] = pool_own[...]
    copy = push(pool_own, pool_pair.at[c], pair_s.at[9], pair_r.at[9], {"seq": partner})
    copy.wait_recv()
    pool_pair_sum[...] = pool_pair[0] + pool_pair[1]
    pool_plane[y] = pool_pair_sum[...]
    copies = [
        push(pool_pair_sum, pool_plane.at[y], plane_s.at[9 + k], plane_r.at[9 + k], {"seq": to_y[k]})
        for k in (2, 1, 3)
    ]
    for copy in copies:
        copy.wait_recv()
    pool_plane_sum[...] = (pool_plane[0] + pool_plane[1]) + (pool_plane[2] + pool_plane[3])
    pool_axis[z] = pool_plane_sum[...]
    copies = [
        push(pool_plane_sum, pool_axis.at[z], axis_s.at[24 + k], axis_r.at[24 + k], {"seq": to_z[k]})
        for k in (4, 5, 3, 6, 2, 7, 1)
    ]
    for copy in copies:
        copy.wait_recv()
    pooled = pool_axis[0]
    for q in range(1, NZ):
        pooled = pooled + pool_axis[q]
    pooled = pooled / (G * NZ * NY * NC)
    square = jnp.sum(pooled * pooled, keepdims=True) / (TILES * L)
    normed = (pooled / jnp.sqrt(square + EPS)).astype(BF16)
    for copy in table_copies:
        copy.wait_recv()
    own_rows.wait()
    wide = jnp.concatenate(
        [jnp.broadcast_to(normed[j : j + 1, :], (16, L)) for j in range(TILES)], axis=1
    )
    classifier = table[...].reshape(TILES * L, L)
    logits = jnp.dot(wide, classifier, preferred_element_type=F32)
    logits_ref[...] = logits[0:1, :]

    for copy in sends:
        copy.wait_send()


def local(inputs, keys_queries, log_decay, skip, classifier):
    copies, positions, channels = inputs.shape
    heads = log_decay.shape[1]
    vm = pl.BlockSpec(memory_space=pltpu.VMEM)
    state = (NY, NZ, ROWS, L)
    scratch = [
        pltpu.VMEM((TILES, G, L), F32),
        pltpu.VMEM((TILES, G, L), F32),
        pltpu.VMEM((NC, *state), BF16),
        pltpu.VMEM(state, BF16),
        pltpu.VMEM(state, BF16),
        pltpu.VMEM(state, BF16),
        pltpu.VMEM(state, F32),
        pltpu.VMEM((NZ, ROWS, L), BF16),
        pltpu.VMEM((NZ, ROWS, L), BF16),
        pltpu.VMEM((NZ, ROWS, L), BF16),
        pltpu.VMEM((NZ, ROWS, L), BF16),
        pltpu.VMEM(state, BF16),
        pltpu.VMEM(state, BF16),
        pltpu.VMEM((NC, *state), BF16),
        pltpu.VMEM(state, BF16),
        pltpu.VMEM((NX, *classifier.shape), BF16),
        pltpu.VMEM((NY, 8, L), F32),
        pltpu.VMEM((NY, 8, L), F32),
        pltpu.VMEM((NY, 8, L), F32),
        pltpu.VMEM((NY, 8, L), F32),
        pltpu.VMEM((8, L), F32),
        pltpu.VMEM((NZ, 8, L), F32),
        pltpu.VMEM((4, NY, ROWS, L), F32),
        pltpu.VMEM((NY, ROWS, L), F32),
        pltpu.VMEM((32, L), F32),
        pltpu.VMEM((NC, 32, L), F32),
        pltpu.VMEM((32, L), F32),
        pltpu.VMEM((NY, 32, L), F32),
        pltpu.VMEM((32, L), F32),
        pltpu.VMEM((NZ, 32, L), F32),
        pltpu.SemaphoreType.DMA((10,)),
        pltpu.SemaphoreType.DMA((10,)),
        pltpu.SemaphoreType.DMA((13,)),
        pltpu.SemaphoreType.DMA((13,)),
        pltpu.SemaphoreType.DMA((32,)),
        pltpu.SemaphoreType.DMA((32,)),
        pltpu.SemaphoreType.DMA((4,)),
        pltpu.SemaphoreType.DMA((4,)),
        pltpu.SemaphoreType.DMA,
    ]
    mixed, logits = pl.pallas_call(
        kernel,
        out_shape=(
            jax.ShapeDtypeStruct((positions, channels), BF16),
            jax.ShapeDtypeStruct((1, classifier.shape[1]), F32),
        ),
        in_specs=[vm, vm, vm, pl.BlockSpec(memory_space=pltpu.SMEM), vm],
        out_specs=(vm, vm),
        scratch_shapes=scratch,
        compiler_params=pltpu.CompilerParams(
            collective_id=0, has_side_effects=True, vmem_limit_bytes=48 << 20
        ),
    )(
        inputs.reshape(positions, channels),
        keys_queries.reshape(positions, 2 * N),
        log_decay.reshape(heads, positions),
        skip,
        classifier,
    )
    return mixed.reshape(copies, positions, channels), logits


def solution(mesh):
    return jax.shard_map(
        local,
        mesh=mesh,
        in_specs=(
            P("fsdp", "seq", None),
            P("fsdp", "seq", None),
            P("fsdp", None, "seq"),
            P(),
            P("fsdp", None),
        ),
        out_specs=(P("fsdp", "seq", None), P("fsdp", None)),
        check_vma=False,
    )
```

time: 500 us -> 55.8 us (0.11)
  the two profiles are of different devices: /device:TPU:2 before, /device:TPU:4 now
where the time goes in v1:
time: 55.8 us; the launch traced here: 55.5 us
  Pallas kernels  49.1 us (88%)
  local copies, waits for them, and re-layouts  5.79 us (10%)
  between operations  0.65 us (1%)
    pallas_call x1, Pallas kernels, local(): pl.pallas_call(kernel, out_shape=(jax.ShapeDtypeStruct((positions, channe...  49.1 us
    unnamed x12, local copies, waits for them, and re-layouts  5.79 us

profile of v1, /device:TPU:4, one launch (start us, length us, event | category | flops | bytes accessed | tf_op | source)
XLA Modules:
  0.0 55.5 jit_solution(6754826300842030471)
XLA Ops:
  0.6 0.0 copy-start.4
  0.6 0.6 %copy-done.4 = f32[56]{0:T(128)S(1)} copy-done((f32[56]{0:T(128)S(1)}, f32[56]{0:T(128)}, u32[]{:S(2)}) %copy-start.4) | copy-done | bytes 248
  1.3 0.0 copy-start
  1.3 1.2 %copy-done = bf16[1,128,3584]{2,1,0:T(8,128)(2,1)S(1)} copy-done((bf16[1,128,3584]{2,1,0:T(8,128)(2,1)S(1)}, bf16[1,128,3584]{2,1,0:T(8,128)(2,1)}, u32[]{:S(2)}) %copy-start) | copy-done | bytes 917528
  2.5 0.0 copy-start.1
  2.5 0.9 %copy-done.1 = bf16[896,128]{1,0:T(8,128)(2,1)S(1)} copy-done((bf16[896,128]{1,0:T(8,128)(2,1)S(1)}, bf16[896,128]{1,0:T(8,128)(2,1)}, u32[]{:S(2)}) %copy-start.1) | copy-done | bytes 229400
  3.4 0.0 copy-start.2
  3.4 0.8 %copy-done.2 = bf16[1,128,256]{2,1,0:T(8,128)(2,1)S(1)} copy-done((bf16[1,128,256]{2,1,0:T(8,128)(2,1)S(1)}, bf16[1,128,256]{2,1,0:T(8,128)(2,1)}, u32[]{:S(2)}) %copy-start.2) | copy-done | bytes 65560
  4.2 0.0 copy-start.3
  4.2 0.7 %copy-done.3 = f32[1,56,128]{2,1,0:T(8,128)S(1)} copy-done((f32[1,56,128]{2,1,0:T(8,128)S(1)}, f32[1,56,128]{2,1,0:T(8,128)}, u32[]{:S(2)}) %copy-start.3) | copy-done | bytes 28696
  5.0 49.1 %shard_map.68 = (bf16[128,3584]{1,0:T(8,128)(2,1)S(1)}, f32[1,128]{1,0:T(1,128)S(1)}) custom-call(bf16[128,3584]{1,0:T(8,128)(2,1)S(1)} %bitcast.5, bf16[128,256]{1,0:T(8,128)(2,1)S(1)} %bitcast.6, f32[56,128]{1,0:T(8,128)S(1)} %bitcast.7, f32[56]{0:T(128)S(1)} %copy-done.4, bf16[896,128]{1,0:T(8,128)(2,1)S(1)} %copy-done.1), custom_call_target="tpu_custom_call" | custom-call | tf_op jit(solution)/shard_map/pallas_call | solution.py:367
  54.1 0.9 %copy.9 = bf16[1,128,3584]{2,1,0:T(8,128)(2,1)} copy(bf16[1,128,3584]{2,1,0:T(8,128)(2,1)S(1)} %bitcast.4) | data formatting | bytes 1835008
  55.0 0.5 copy.10
Async XLA Ops:
  0.6 0.7 %copy-start.4 = (f32[56]{0:T(128)S(1)}, f32[56]{0:T(128)}, u32[]{:S(2)}) copy-start(f32[56]{0:T(128)} %skip_ref.1) | copy-start | bytes 676
  1.3 1.2 %copy-start = (bf16[1,128,3584]{2,1,0:T(8,128)(2,1)S(1)}, bf16[1,128,3584]{2,1,0:T(8,128)(2,1)}, u32[]{:S(2)}) copy-start(bf16[1,128,3584]{2,1,0:T(8,128)(2,1)} %param.5) | copy-start | bytes 2752516
  2.5 0.9 %copy-start.1 = (bf16[896,128]{1,0:T(8,128)(2,1)S(1)}, bf16[896,128]{1,0:T(8,128)(2,1)}, u32[]{:S(2)}) copy-start(bf16[896,128]{1,0:T(8,128)(2,1)} %cls_ref.1) | copy-start | bytes 688132
  3.4 0.8 %copy-start.2 = (bf16[1,128,256]{2,1,0:T(8,128)(2,1)S(1)}, bf16[1,128,256]{2,1,0:T(8,128)(2,1)}, u32[]{:S(2)}) copy-start(bf16[1,128,256]{2,1,0:T(8,128)(2,1)} %param.6) | copy-start | bytes 196612
  4.2 0.7 %copy-start.3 = (f32[1,56,128]{2,1,0:T(8,128)S(1)}, f32[1,56,128]{2,1,0:T(8,128)}, u32[]{:S(2)}) copy-start(f32[1,56,128]{2,1,0:T(8,128)} %param.7) | copy-start | bytes 86020

commit v2 on v1

v2 whole, which is shorter than its diff:
```python
import jax
import jax.numpy as jnp
from jax import lax
from jax.experimental import pallas as pl
from jax.experimental.pallas import tpu as pltpu
from jax.sharding import PartitionSpec as P

MESH = pl.DeviceIdType.MESH
F32, BF16 = jnp.float32, jnp.bfloat16
HIGHEST = lax.Precision.HIGHEST

N = 128
G = 128
L = 128
NZ, NY, NC, NX = 8, 4, 2, 4
HEADS = 56
TILES = 28
M = TILES // NY
CHUNKS = ((0, 4), (4, 3))
NCH = len(CHUNKS)
EPS = 1e-06
FAR_Y = (2, 1, 3)
FAR_Z = (4, 5, 3, 6, 2, 7, 1)


def spread(x):
    return jnp.concatenate(
        [jnp.broadcast_to(x[m : m + 1, :], (8, L)) for m in range(M)], axis=0
    )


def kernel(
    v_hbm, kq_hbm, ld_hbm, skip_ref, cls_ref, mixed_ref, logits_ref,
    v_ref, kq_ref, ld_ref, out_ref, grow, local_out, table,
    decay_own, decay_pair, decay_chip, decay_plane, decay_sum, decay_axis,
    pair_factor, start_factor, plane_factor, plane_start, axis_factor,
    response, response_pair, pool_local, pool_own, pool_plane, pool_sum, pool_axis,
    *rest,
):
    buffers = [rest[i * 12 : (i + 1) * 12] for i in range(NCH)]
    (in_s, out_s, pair_s, pair_r, plane_s, plane_r, axis_s, axis_r,
     back_s, back_r, table_s, table_r, small_s, small_r) = rest[NCH * 12 :]
    me, x = lax.axis_index("seq"), lax.axis_index("fsdp")
    c = lax.rem(me, NC)
    y = lax.rem(me // NC, NY)
    z = me // (NC * NY)
    other = 1 - c
    ys = [lax.rem(y + k, NY) for k in range(NY)]
    zs = [lax.rem(z + k, NZ) for k in range(NZ)]

    def at(z_, y_, c_):
        return {"seq": (z_ * NY + y_) * NC + c_}

    to_pair = at(z, y, other)
    to_y = [at(z, ys[k], c) for k in range(NY)]
    to_y_other = [at(z, ys[k], other) for k in range(NY)]
    to_z = [at(zs[k], y, c) for k in range(NZ)]
    to_x = [{"fsdp": lax.rem(x + k, NX)} for k in range(NX)]

    barrier = pltpu.get_barrier_semaphore()
    partners = to_z[1:] + to_y[1:] + to_y_other[1:] + to_x[1:] + [to_pair]
    for who in partners:
        pl.semaphore_signal(barrier, inc=1, device_id=who, device_id_type=MESH)

    loads = [
        pltpu.make_async_copy(src, dst, in_s.at[i])
        for i, (src, dst) in enumerate(
            ((ld_hbm, ld_ref), (kq_hbm, kq_ref), (v_hbm, v_ref), (cls_ref, table.at[x]))
        )
    ]
    for load in loads:
        load.start()

    sends = []

    def push(src, dst, send, recv, who):
        copy = pltpu.make_async_remote_copy(
            src_ref=src, dst_ref=dst, send_sem=send, recv_sem=recv,
            device_id=who, device_id_type=MESH,
        )
        copy.start()
        sends.append(copy)
        return copy

    loads[0].wait()
    left_half = lax.broadcasted_iota(jnp.int32, (1, L), 1) < 64
    for g in range(NY):
        even = jnp.sum(ld_ref[pl.ds(2 * M * g, M, stride=2), :], axis=1, keepdims=True)
        odd = jnp.sum(ld_ref[pl.ds(2 * M * g + 1, M, stride=2), :], axis=1, keepdims=True)
        decay_own[g, 0:M, :] = jnp.where(left_half, even, odd)
        decay_own[g, M:8, :] = jnp.zeros((8 - M, L), F32)

    row = lax.broadcasted_iota(jnp.int32, (G, G), 0)
    col = lax.broadcasted_iota(jnp.int32, (G, G), 1)
    causal = row >= col
    lower = jnp.where(causal, 1.0, 0.0).astype(F32)
    log_decay = ld_ref[...]
    cum = lax.dot_general(
        log_decay, lower, (((1,), (1,)), ((), ())), precision=HIGHEST, preferred_element_type=F32
    )
    cum_t = lax.dot_general(
        lower, log_decay, (((1,), (1,)), ((), ())), precision=HIGHEST, preferred_element_type=F32
    )
    loads[1].wait()
    keys = kq_ref[:, :N]
    queries = kq_ref[:, N:]
    keys_t = keys.T
    loads[2].wait()

    def state_of(i):
        first, count = CHUNKS[i]
        state = buffers[i][0]
        for g in range(NY):
            for m in range(count):
                j = g * M + first + m
                lanes = slice(j * L, (j + 1) * L)
                level = jnp.where(
                    left_half, cum_t[:, 2 * j : 2 * j + 1], cum_t[:, 2 * j + 1 : 2 * j + 2]
                )
                grow[j] = level
                weight = jnp.exp(level[G - 1 : G, :] - level)
                weighted = (v_ref[:, lanes].astype(F32) * weight).astype(BF16)
                value = jnp.dot(keys_t, weighted, preferred_element_type=F32).astype(BF16)
                for half in range(NC):
                    to = jnp.where(c == half, c, 2)
                    for b in range(NZ):
                        at_row = half * 64 + b * 8
                        state[to, g, b, m * 8 : m * 8 + 8, :] = value[at_row : at_row + 8, :]

    def send_half(i):
        state = buffers[i][0]
        return push(state.at[2], state.at[c], pair_s.at[i], pair_r.at[i], to_pair)

    def inside(g):
        scores = lax.dot_general(
            queries, keys, (((1,), (1,)), ((), ())), preferred_element_type=F32
        )
        scores = jnp.where(causal, scores, 0.0)
        for m in range(M):
            j = g * M + m
            lanes = slice(j * L, (j + 1) * L)
            parts = []
            for h in (2 * j, 2 * j + 1):
                gap = jnp.minimum(cum_t[:, h : h + 1] - cum[h : h + 1, :], 0.0)
                parts.append((scores * jnp.exp(gap)).astype(BF16))
            value = v_ref[:, lanes]
            zero = jnp.zeros_like(value)
            stacked = jnp.concatenate(
                [jnp.where(left_half, value, zero), jnp.where(left_half, zero, value)], axis=0
            )
            diagonal = jnp.dot(
                jnp.concatenate(parts, axis=1), stacked, preferred_element_type=F32
            )
            direct = jnp.where(left_half, skip_ref[2 * j], skip_ref[2 * j + 1])
            result = diagonal + direct * value.astype(F32)
            local_out[j] = result
            pool_local[j : j + 1, :] = jnp.sum(result, axis=0, keepdims=True)
            grow[j] = jnp.exp(grow[j])

    pool_local[TILES:32, :] = jnp.zeros((32 - TILES, L), F32)
    state_of(0)
    pl.semaphore_wait(barrier, len(partners))
    pair_decay = push(decay_own, decay_pair, small_s.at[0], small_r.at[0], to_pair)
    pair_copies = [send_half(0)]
    for i in range(1, NCH):
        state_of(i)
        pair_copies.append(send_half(i))
    response[0] = lax.dot_general(
        jnp.exp(cum_t), queries.astype(F32), (((0,), (0,)), ((), ())),
        precision=HIGHEST, preferred_element_type=F32,
    )
    response[1] = jnp.broadcast_to(jnp.sum(log_decay, axis=1, keepdims=True), (HEADS, L))
    pair_response = push(response, response_pair, small_s.at[1], small_r.at[1], to_pair)
    table_copies = [
        push(cls_ref, table.at[x], table_s.at[k], table_r.at[k], to_x[k]) for k in range(1, NX)
    ]
    inside(0)

    pair_decay.wait_recv()
    for g in range(NY):
        mine, theirs = decay_own[g], decay_pair[g]
        decay_chip[g] = mine + theirs
        pair_factor[g] = spread(jnp.exp(jnp.where(c == 0, theirs, mine)))
        start_factor[g] = spread(jnp.exp(jnp.where(c == 0, mine, theirs)))
    plane_decays = [
        push(decay_chip.at[ys[k]], decay_plane.at[y], small_s.at[1 + k], small_r.at[1 + k], to_y[k])
        for k in FAR_Y
    ]
    decay_plane[y] = decay_chip[y]

    plane_copies = [[] for _ in CHUNKS]
    for i, (first, count) in enumerate(CHUNKS):
        state, pair_total, plane_recv = buffers[i][:3]
        rows = slice(first * 8, (first + count) * 8)
        pair_copies[i].wait_recv()
        for k in (*FAR_Y, 0):
            g = ys[k]

            @pl.loop(0, NZ)
            def _(b, g=g, k=k):
                total = pair_factor[g, rows, :] * state[0, g, b].astype(F32) + state[1, g, b].astype(F32)
                if k == 0:
                    plane_recv[y, b] = total.astype(BF16)
                else:
                    pair_total[k, b] = total.astype(BF16)

            if k:
                plane_copies[i].append(
                    push(pair_total.at[k], plane_recv.at[y], plane_s.at[i, k], plane_r.at[i, k], to_y[k])
                )

    inside(1)
    for copy in plane_decays:
        copy.wait_recv()
    run = jnp.zeros((8, L), F32)
    for k in range(NY):
        plane_factor[k] = spread(jnp.exp(decay_plane[k]))
        plane_start[k] = spread(jnp.exp(run))
        run = run + decay_plane[k]
    decay_sum[...] = run
    decay_axis[z] = run
    axis_decays = [
        push(decay_sum, decay_axis.at[z], small_s.at[4 + k], small_r.at[4 + k], to_z[k])
        for k in FAR_Z
    ]
    inside(2)

    axis_copies = [[] for _ in CHUNKS]
    for i, (first, count) in enumerate(CHUNKS):
        plane_recv, plane_prefix, axis_send, axis_recv = buffers[i][2:6]
        rows = slice(first * 8, (first + count) * 8)
        for copy in plane_copies[i]:
            copy.wait_recv()
        for k in (*FAR_Z, 0):
            b = zs[k]
            total = jnp.zeros((count * 8, L), F32)
            for q in range(NY):
                plane_prefix[q, b] = total
                total = plane_factor[q, rows, :] * total + plane_recv[q, b].astype(F32)
            if k == 0:
                axis_recv[z] = total.astype(BF16)
            else:
                axis_send[k] = total.astype(BF16)
                axis_copies[i].append(
                    push(axis_send.at[k], axis_recv.at[z], axis_s.at[i, k], axis_r.at[i, k], to_z[k])
                )
    inside(3)
    for copy in axis_decays:
        copy.wait_recv()
    for q in range(NZ):
        axis_factor[q] = spread(jnp.exp(decay_axis[q]))
    pair_response.wait_recv()
    resp_0 = jnp.where(c == 0, response[0], response_pair[0])
    resp_1 = jnp.where(c == 0, response_pair[0], response[0])
    resp_0 = resp_0 + jnp.exp(jnp.where(c == 0, response[1], response_pair[1])) * resp_1
    turned_0, turned_1 = pltpu.roll(resp_0, 64, 1), pltpu.roll(resp_1, 64, 1)
    both = jnp.where(
        c == 0, jnp.where(left_half, resp_0, turned_1), jnp.where(left_half, turned_0, resp_1)
    )
    both_high = both.astype(BF16)
    both_low = (both - both_high.astype(F32)).astype(BF16)
    half_queries = jnp.where(
        c == 0, queries.astype(F32), pltpu.roll(queries.astype(F32), 64, 1)
    ).astype(BF16)

    back_copies = [[] for _ in CHUNKS]
    for i, (first, count) in enumerate(CHUNKS):
        axis_recv, axis_prefix, start_plane = buffers[i][5:8]
        rows = slice(first * 8, (first + count) * 8)
        for copy in axis_copies[i]:
            copy.wait_recv()
        total = jnp.zeros((count * 8, L), F32)
        for q in range(NZ):
            axis_prefix[q] = total.astype(BF16)
            if q < NZ - 1:
                total = axis_factor[q, rows, :] * total + axis_recv[q].astype(F32)
        back_copies[i] = [
            push(axis_prefix.at[zs[k]], start_plane.at[z], back_s.at[i, k], back_r.at[i, k], to_z[k])
            for k in FAR_Z
        ]
        start_plane[z] = axis_prefix[z]

    chip_copies = [[] for _ in CHUNKS]
    for i, (first, count) in enumerate(CHUNKS):
        plane_prefix = buffers[i][3]
        start_plane, start_send, start_chip = buffers[i][7:10]
        rows = slice(first * 8, (first + count) * 8)
        for copy in back_copies[i]:
            copy.wait_recv()
        for k in (*FAR_Y, 0):
            g = ys[k]

            @pl.loop(0, NZ)
            def _(b, g=g, k=k):
                start = plane_start[g, rows, :] * start_plane[b].astype(F32) + plane_prefix[g, b]
                if k == 0:
                    start_chip[y, b] = start.astype(BF16)
                else:
                    start_send[k, b] = start.astype(BF16)

            if k:
                chip_copies[i].append(
                    push(start_send.at[k], start_chip.at[y], plane_s.at[i, 3 + k], plane_r.at[i, 3 + k], to_y[k])
                )

    half_copies = []
    for i, (first, count) in enumerate(CHUNKS):
        state = buffers[i][0]
        start_chip, carried, carried_recv = buffers[i][9:12]
        rows = slice(first * 8, (first + count) * 8)
        for copy in chip_copies[i]:
            copy.wait_recv()

        @pl.loop(0, NY)
        def _(g):
            @pl.loop(0, NZ)
            def _(b):
                before = start_chip[g, b].astype(F32)
                after = start_factor[g, rows, :] * before + state[0, g, b].astype(F32)
                carried[0, g, b] = start_chip[g, b]
                carried[1, g, b] = after.astype(BF16)

        half_copies.append(
            push(carried.at[other], carried_recv, pair_s.at[NCH + i], pair_r.at[NCH + i], to_pair)
        )
        for g in range(NY):
            for m in range(count):
                j = g * M + first + m
                tile = slice(m * 8, m * 8 + 8)
                start = jnp.concatenate(
                    [start_chip[g, b, tile, :] for b in range(NZ)]
                    + [state[0, g, b, tile, :] for b in range(NZ)],
                    axis=0,
                )
                added = jnp.dot(both_high, start, preferred_element_type=F32) + jnp.dot(
                    both_low, start, preferred_element_type=F32
                )
                pool_own[j : j + 1, :] = pool_local[j : j + 1, :] + jnp.where(
                    left_half, added[2 * j : 2 * j + 1, :], added[2 * j + 1 : 2 * j + 2, :]
                )

    pool_own[TILES:32, :] = pool_local[TILES:32, :]
    pool_plane[y * NC + c] = pool_own[...]
    mine = pool_plane.at[y * NC + c]
    pool_copies = (
        [push(pool_own, mine, small_s.at[11 + k], small_r.at[11 + k], to_y[k]) for k in FAR_Y]
        + [push(pool_own, mine, small_s.at[14 + k], small_r.at[14 + k], to_y_other[k]) for k in FAR_Y]
        + [push(pool_own, mine, small_s.at[18], small_r.at[18], to_pair)]
    )

    stores = []

    def final(i):
        first, count = CHUNKS[i]
        carried, carried_recv = buffers[i][10:12]
        half_copies[i].wait_recv()
        for g in range(NY):
            for m in range(count):
                j = g * M + first + m
                lanes = slice(j * L, (j + 1) * L)
                tile = slice(m * 8, m * 8 + 8)
                start = jnp.concatenate(
                    [carried[c, g, b, tile, :] for b in range(NZ)]
                    + [carried_recv[g, b, tile, :] for b in range(NZ)],
                    axis=0,
                )
                full = local_out[j] + grow[j] * jnp.dot(
                    half_queries, start, preferred_element_type=F32
                )
                out_ref[:, lanes] = full.astype(BF16)
            lanes = slice((g * M + first) * L, (g * M + first + count) * L)
            store = pltpu.make_async_copy(
                out_ref.at[:, lanes], mixed_ref.at[:, lanes], out_s.at[i * NY + g]
            )
            store.start()
            stores.append(store)

    def sum_plane():
        for copy in pool_copies:
            copy.wait_recv()
        total = pool_plane[0]
        for q in range(1, NY * NC):
            total = total + pool_plane[q]
        pool_sum[...] = total
        pool_axis[z] = total
        return [
            push(pool_sum, pool_axis.at[z], small_s.at[18 + k], small_r.at[18 + k], to_z[k])
            for k in FAR_Z
        ]

    if NCH == 1:
        last_copies = sum_plane()
        final(0)
    else:
        final(0)
        last_copies = sum_plane()
        for i in range(1, NCH):
            final(i)

    for copy in table_copies:
        copy.wait_recv()
    loads[3].wait()
    for copy in last_copies:
        copy.wait_recv()
    pooled = pool_axis[0]
    for q in range(1, NZ):
        pooled = pooled + pool_axis[q]
    pooled = pooled / (G * NZ * NY * NC)
    square = jnp.sum(pooled * pooled, keepdims=True) / (TILES * L)
    normed = (pooled / jnp.sqrt(square + EPS)).astype(BF16)
    wide = jnp.concatenate(
        [jnp.broadcast_to(normed[j : j + 1, :], (16, L)) for j in range(TILES)], axis=1
    )
    classifier = table[...].reshape(TILES * L, L)
    logits = jnp.dot(wide, classifier, preferred_element_type=F32)
    logits_ref[...] = logits[0:1, :]

    for store in stores:
        store.wait()
    for copy in sends:
        copy.wait_send()


def local(inputs, keys_queries, log_decay, skip, classifier):
    copies, positions, channels = inputs.shape
    heads = log_decay.shape[1]
    hbm = pl.BlockSpec(memory_space=pltpu.HBM)

    def chunk(count):
        slab = (NZ, count * 8, L)
        return [
            pltpu.VMEM((3, NY, *slab), BF16),
            pltpu.VMEM((NY, *slab), BF16),
            pltpu.VMEM((NY, *slab), BF16),
            pltpu.VMEM((NY, *slab), F32),
            pltpu.VMEM(slab, BF16),
            pltpu.VMEM(slab, BF16),
            pltpu.VMEM(slab, BF16),
            pltpu.VMEM(slab, BF16),
            pltpu.VMEM((NY, *slab), BF16),
            pltpu.VMEM((NY, *slab), BF16),
            pltpu.VMEM((NC, NY, *slab), BF16),
            pltpu.VMEM((NY, *slab), BF16),
        ]

    dma = pltpu.SemaphoreType.DMA
    scratch = [
        pltpu.VMEM((positions, channels), BF16),
        pltpu.VMEM((positions, 2 * N), BF16),
        pltpu.VMEM((heads, positions), F32),
        pltpu.VMEM((positions, channels), BF16),
        pltpu.VMEM((TILES, G, L), F32),
        pltpu.VMEM((TILES, G, L), F32),
        pltpu.VMEM((NX, *classifier.shape), BF16),
        pltpu.VMEM((NY, 8, L), F32),
        pltpu.VMEM((NY, 8, L), F32),
        pltpu.VMEM((NY, 8, L), F32),
        pltpu.VMEM((NY, 8, L), F32),
        pltpu.VMEM((8, L), F32),
        pltpu.VMEM((NZ, 8, L), F32),
        pltpu.VMEM((NY, M * 8, L), F32),
        pltpu.VMEM((NY, M * 8, L), F32),
        pltpu.VMEM((NY, M * 8, L), F32),
        pltpu.VMEM((NY, M * 8, L), F32),
        pltpu.VMEM((NZ, M * 8, L), F32),
        pltpu.VMEM((2, HEADS, L), F32),
        pltpu.VMEM((2, HEADS, L), F32),
        pltpu.VMEM((32, L), F32),
        pltpu.VMEM((32, L), F32),
        pltpu.VMEM((NY * NC, 32, L), F32),
        pltpu.VMEM((32, L), F32),
        pltpu.VMEM((NZ, 32, L), F32),
        *[ref for _, count in CHUNKS for ref in chunk(count)],
        dma((4,)), dma((NCH * NY,)),
        dma((2 * NCH,)), dma((2 * NCH,)), dma((NCH, 7)), dma((NCH, 7)),
        dma((NCH, NZ)), dma((NCH, NZ)), dma((NCH, NZ)), dma((NCH, NZ)),
        dma((NX,)), dma((NX,)), dma((26,)), dma((26,)),
    ]
    mixed, logits = pl.pallas_call(
        kernel,
        out_shape=(
            jax.ShapeDtypeStruct((positions, channels), BF16),
            jax.ShapeDtypeStruct((1, classifier.shape[1]), F32),
        ),
        in_specs=[hbm, hbm, hbm, pl.BlockSpec(memory_space=pltpu.SMEM), hbm],
        out_specs=(hbm, pl.BlockSpec(memory_space=pltpu.VMEM)),
        scratch_shapes=scratch,
        compiler_params=pltpu.CompilerParams(
            collective_id=0, has_side_effects=True, vmem_limit_bytes=60 << 20
        ),
    )(
        inputs.reshape(positions, channels),
        keys_queries.reshape(positions, 2 * N),
        log_decay.reshape(heads, positions),
        skip,
        classifier,
    )
    return mixed.reshape(copies, positions, channels), logits


def solution(mesh):
    return jax.shard_map(
        local,
        mesh=mesh,
        in_specs=(
            P("fsdp", "seq", None),
            P("fsdp", "seq", None),
            P("fsdp", None, "seq"),
            P(),
            P("fsdp", None),
        ),
        out_specs=(P("fsdp", "seq", None), P("fsdp", None)),
        check_vma=False,
    )
```

time: 55.8 us -> 48.2 us (0.86)
  the two profiles are of different devices: /device:TPU:4 before, /device:TPU:1 now
where the time goes in v2:
time: 48.2 us; the launch traced here: 48.1 us
  Pallas kernels  44.8 us (93%)
  local copies, waits for them, and re-layouts  2.68 us (6%)
  between operations  0.65 us (1%)
    pallas_call x1, Pallas kernels, local(): pl.pallas_call(kernel, out_shape=(jax.ShapeDtypeStruct((positions, channe...  44.8 us
    unnamed x4, local copies, waits for them, and re-layouts  2.68 us

profile of v2, /device:TPU:1, one launch (start us, length us, event | category | flops | bytes accessed | tf_op | source)
XLA Modules:
  0.0 48.1 jit_solution(17170266960857003917)
XLA Ops:
  0.6 44.8 %shard_map.68 = (bf16[128,3584]{1,0:T(8,128)(2,1)}, f32[1,128]{1,0:T(1,128)}) custom-call(bf16[128,3584]{1,0:T(8,128)(2,1)} %bitcast.5, bf16[128,256]{1,0:T(8,128)(2,1)} %bitcast.6, f32[56,128]{1,0:T(8,128)} %bitcast.7, f32[56]{0:T(128)} %skip_ref.1, bf16[896,128]{1,0:T(8,128)(2,1)} %cls_ref.1), custom_call_target="tpu_custom_call" | custom-call | tf_op jit(solution)/shard_map/pallas_call | solution.py:479
  45.4 0.0 copy-start
  45.4 2.2 %copy.9 = bf16[1,128,3584]{2,1,0:T(8,128)(2,1)} copy(bf16[1,128,3584]{2,1,0:T(8,128)(2,1)} %bitcast.4) | data formatting | bytes 1835008
  47.6 0.0 copy-done
  47.6 0.5 %copy.10 = f32[1,128]{1,0:T(1,128)} copy(f32[1,128]{1,0:T(1,128)S(1)} %copy-done) | data formatting | bytes 1024
Async XLA Ops:
  45.4 2.2 %copy-start = (f32[1,128]{1,0:T(1,128)S(1)}, f32[1,128]{1,0:T(1,128)}, u32[]{:S(2)}) copy-start(f32[1,128]{1,0:T(1,128)} %get-tuple-element.9) | copy-start | bytes 1540

commit v3 on v2

--- a/solution.py
+++ b/solution.py
@@ -32,9 +32,10 @@
 def kernel(
     v_hbm, kq_hbm, ld_hbm, skip_ref, cls_ref, mixed_ref, logits_ref,
     v_ref, kq_ref, ld_ref, out_ref, grow, local_out, table,
-    decay_own, decay_pair, decay_chip, decay_plane, decay_sum, decay_axis,
+    decay_own, decay_pair, decay_chip, decay_plane,
     pair_factor, start_factor, plane_factor, plane_start, axis_factor,
-    response, response_pair, pool_local, pool_own, pool_plane, pool_sum, pool_axis,
+    response, response_pair, chip_response, plane_response, axis_note, axis_notes,
+    pool_own, pool_parts, pool_send, pool_axis, pool_sum, pool_plane,
     *rest,
 ):
     buffers = [rest[i * 12 : (i + 1) * 12] for i in range(NCH)]
@@ -106,6 +107,19 @@
     queries = kq_ref[:, N:]
     keys_t = keys.T
     loads[2].wait()
+
+    def pool_rows(responses, parts, first, count):
+        whole = jnp.concatenate(responses, axis=1)
+        high = whole.astype(BF16)
+        low = (whole - high.astype(F32)).astype(BF16)
+        both = jnp.concatenate([high, low], axis=0)
+        made = []
+        for m in range(count):
+            t = 2 * (first + m)
+            added = jnp.dot(both, jnp.concatenate(parts(m), axis=0), preferred_element_type=F32)
+            added = added[0 : 2 * M, :] + added[2 * M : 4 * M, :]
+            made.append(jnp.where(left_half, added[t : t + 1, :], added[t + 1 : t + 2, :]))
+        return jnp.concatenate(made, axis=0)
 
     def state_of(i):
         first, count = CHUNKS[i]
@@ -154,10 +168,11 @@
             direct = jnp.where(left_half, skip_ref[2 * j], skip_ref[2 * j + 1])
             result = diagonal + direct * value.astype(F32)
             local_out[j] = result
-            pool_local[j : j + 1, :] = jnp.sum(result, axis=0, keepdims=True)
+            pool_own[g, m : m + 1, :] = jnp.sum(result, axis=0, keepdims=True)
             grow[j] = jnp.exp(grow[j])
 
-    pool_local[TILES:32, :] = jnp.zeros((32 - TILES, L), F32)
+    for g in range(NY):
+        pool_own[g, M:8, :] = jnp.zeros((8 - M, L), F32)
     state_of(0)
     pl.semaphore_wait(barrier, len(partners))
     pair_decay = push(decay_own, decay_pair, small_s.at[0], small_r.at[0], to_pair)
@@ -209,21 +224,59 @@
                     push(pair_total.at[k], plane_recv.at[y], plane_s.at[i, k], plane_r.at[i, k], to_y[k])
                 )
 
+    pair_response.wait_recv()
+    resp_0 = jnp.where(c == 0, response[0], response_pair[0])
+    resp_1 = jnp.where(c == 0, response_pair[0], response[0])
+    resp_0 = resp_0 + jnp.exp(jnp.where(c == 0, response[1], response_pair[1])) * resp_1
+    chip_decay = response[1] + response_pair[1]
+    for g in range(NY):
+        heads = slice(2 * M * g, 2 * M * (g + 1))
+        chip_response[g, 0, 0 : 2 * M, :] = resp_0[heads, :]
+        chip_response[g, 1, 0 : 2 * M, :] = chip_decay[heads, :]
+        chip_response[g, :, 2 * M : 16, :] = jnp.zeros((2, 16 - 2 * M, L), F32)
+    plane_responses = [
+        push(chip_response.at[ys[k]], plane_response.at[y], small_s.at[4 + k], small_r.at[4 + k], to_y[k])
+        for k in FAR_Y
+    ]
+    plane_response[y] = chip_response[y]
     inside(1)
-    for copy in plane_decays:
+    for copy in (*plane_decays, *plane_responses):
         copy.wait_recv()
     run = jnp.zeros((8, L), F32)
+    run_head = jnp.zeros((16, L), F32)
+    summed = jnp.zeros((16, L), F32)
     for k in range(NY):
         plane_factor[k] = spread(jnp.exp(decay_plane[k]))
         plane_start[k] = spread(jnp.exp(run))
         run = run + decay_plane[k]
-    decay_sum[...] = run
-    decay_axis[z] = run
-    axis_decays = [
-        push(decay_sum, decay_axis.at[z], small_s.at[4 + k], small_r.at[4 + k], to_z[k])
+        summed = summed + jnp.exp(run_head) * plane_response[k, 0]
+        run_head = run_head + plane_response[k, 1]
+    axis_note[0:8, :] = run
+    axis_note[8:24, :] = summed
+    axis_notes[z, 0:8, :] = run
+    axis_notes[z, 8:24, :] = summed
+    note_copies = [
+        push(axis_note, axis_notes.at[z], small_s.at[7 + k], small_r.at[7 + k], to_z[k])
         for k in FAR_Z
     ]
     inside(2)
+    inside(3)
+    mine_1 = jnp.where(c == 0, resp_1, pltpu.roll(resp_1, 64, 1))
+    for i, (first, count) in enumerate(CHUNKS):
+        state = buffers[i][0]
+        for g in range(NY):
+            group = pool_rows(
+                [mine_1[2 * M * g : 2 * M * (g + 1), 0:64]],
+                lambda m, g=g, state=state: [state[0, g, b, m * 8 : m * 8 + 8, :] for b in range(NZ)],
+                first, count,
+            )
+            tiles = slice(first, first + count)
+            pool_own[g, tiles, :] = pool_own[g, tiles, :] + group
+    part_copies = [
+        push(pool_own.at[ys[k]], pool_parts.at[y], small_s.at[14 + k], small_r.at[14 + k], to_y[k])
+        for k in FAR_Y
+    ]
+    pool_parts[y] = pool_own[y]
 
     axis_copies = [[] for _ in CHUNKS]
     for i, (first, count) in enumerate(CHUNKS):
@@ -244,21 +297,35 @@
                 axis_copies[i].append(
                     push(axis_send.at[k], axis_recv.at[z], axis_s.at[i, k], axis_r.at[i, k], to_z[k])
                 )
-    inside(3)
-    for copy in axis_decays:
+    for copy in part_copies:
         copy.wait_recv()
+    my_half = [
+        jnp.where(c == 0, plane_response[q, 0], pltpu.roll(plane_response[q, 0], 64, 1))[0 : 2 * M, 0:64]
+        for q in range(1, NY)
+    ]
+    pool_rest = (pool_parts[0] + pool_parts[1]) + (pool_parts[2] + pool_parts[3])
+    pool_tiles = []
+    for i, (first, count) in enumerate(CHUNKS):
+        plane_prefix = buffers[i][3]
+        pool_tiles.append(
+            pool_rows(
+                my_half,
+                lambda m, plane_prefix=plane_prefix: [
+                    plane_prefix[q, b, m * 8 : m * 8 + 8, :].astype(BF16)
+                    for q in range(1, NY)
+                    for b in range(NZ)
+                ],
+                first, count,
+            )
+        )
+    for copy in note_copies:
+        copy.wait_recv()
+    lane = lax.broadcasted_iota(jnp.int32, (16, L), 1) // 8
+    my_rows = jnp.zeros((16, L), F32)
     for q in range(NZ):
-        axis_factor[q] = spread(jnp.exp(decay_axis[q]))
-    pair_response.wait_recv()
-    resp_0 = jnp.where(c == 0, response[0], response_pair[0])
-    resp_1 = jnp.where(c == 0, response_pair[0], response[0])
-    resp_0 = resp_0 + jnp.exp(jnp.where(c == 0, response[1], response_pair[1])) * resp_1
-    turned_0, turned_1 = pltpu.roll(resp_0, 64, 1), pltpu.roll(resp_1, 64, 1)
-    both = jnp.where(
-        c == 0, jnp.where(left_half, resp_0, turned_1), jnp.where(left_half, turned_0, resp_1)
-    )
-    both_high = both.astype(BF16)
-    both_low = (both - both_high.astype(F32)).astype(BF16)
+        axis_factor[q] = spread(jnp.exp(axis_notes[q, 0:8, :]))
+        turned = pltpu.roll(axis_notes[q, 8:24, :], lax.rem(2 * L + 8 * q - 64 * c - 8 * z, L), 1)
+        my_rows = my_rows + jnp.where(lane == q, turned, 0.0)
     half_queries = jnp.where(
         c == 0, queries.astype(F32), pltpu.roll(queries.astype(F32), 64, 1)
     ).astype(BF16)
@@ -279,6 +346,23 @@
             for k in FAR_Z
         ]
         start_plane[z] = axis_prefix[z]
+    for i, (first, count) in enumerate(CHUNKS):
+        axis_prefix = buffers[i][6]
+        pool_tiles[i] = pool_tiles[i] + pool_rows(
+            [my_rows[0 : 2 * M, 0:64]],
+            lambda m, axis_prefix=axis_prefix: [
+                axis_prefix[q, m * 8 : m * 8 + 8, :] for q in range(NZ)
+            ],
+            first, count,
+        )
+    pool_send[...] = pool_rest + jnp.concatenate(
+        [*pool_tiles, jnp.zeros((8 - M, L), F32)], axis=0
+    )
+    pool_axis[z] = pool_send[...]
+    pool_copies = [
+        push(pool_send, pool_axis.at[z], small_s.at[17 + k], small_r.at[17 + k], to_z[k])
+        for k in FAR_Z
+    ]
 
     chip_copies = [[] for _ in CHUNKS]
     for i, (first, count) in enumerate(CHUNKS):
@@ -302,6 +386,20 @@
                 chip_copies[i].append(
                     push(start_send.at[k], start_chip.at[y], plane_s.at[i, 3 + k], plane_r.at[i, 3 + k], to_y[k])
                 )
+
+    for copy in pool_copies:
+        copy.wait_recv()
+    total = pool_axis[0]
+    for q in range(1, NZ):
+        total = total + pool_axis[q]
+    pool_sum[...] = total
+    mine = pool_plane.at[y * NC + c]
+    pool_plane[y * NC + c] = total
+    last_copies = (
+        [push(pool_sum, mine, small_s.at[24 + k], small_r.at[24 + k], to_y[k]) for k in FAR_Y]
+        + [push(pool_sum, mine, small_s.at[27 + k], small_r.at[27 + k], to_y_other[k]) for k in FAR_Y]
+        + [push(pool_sum, mine, small_s.at[31], small_r.at[31], to_pair)]
+    )
 
     half_copies = []
     for i, (first, count) in enumerate(CHUNKS):
@@ -323,30 +421,28 @@
         half_copies.append(
             push(carried.at[other], carried_recv, pair_s.at[NCH + i], pair_r.at[NCH + i], to_pair)
         )
-        for g in range(NY):
-            for m in range(count):
-                j = g * M + first + m
-                tile = slice(m * 8, m * 8 + 8)
-                start = jnp.concatenate(
-                    [start_chip[g, b, tile, :] for b in range(NZ)]
-                    + [state[0, g, b, tile, :] for b in range(NZ)],
-                    axis=0,
-                )
-                added = jnp.dot(both_high, start, preferred_element_type=F32) + jnp.dot(
-                    both_low, start, preferred_element_type=F32
-                )
-                pool_own[j : j + 1, :] = pool_local[j : j + 1, :] + jnp.where(
-                    left_half, added[2 * j : 2 * j + 1, :], added[2 * j + 1 : 2 * j + 2, :]
-                )
-
-    pool_own[TILES:32, :] = pool_local[TILES:32, :]
-    pool_plane[y * NC + c] = pool_own[...]
-    mine = pool_plane.at[y * NC + c]
-    pool_copies = (
-        [push(pool_own, mine, small_s.at[11 + k], small_r.at[11 + k], to_y[k]) for k in FAR_Y]
-        + [push(pool_own, mine, small_s.at[14 + k], small_r.at[14 + k], to_y_other[k]) for k in FAR_Y]
-        + [push(pool_own, mine, small_s.at[18], small_r.at[18], to_pair)]
-    )
+
+    for copy in table_copies:
+        copy.wait_recv()
+    loads[3].wait()
+    for copy in last_copies:
+        copy.wait_recv()
+    pooled = [
+        (pool_plane[NC * g] + pool_plane[NC * g + 1]) / (G * NZ * NY * NC) for g in range(NY)
+    ]
+    square = sum(jnp.sum(p * p, keepdims=True) for p in pooled) / (TILES * L)
+    scale = 1.0 / jnp.sqrt(square + EPS)
+    wide = jnp.concatenate(
+        [
+            jnp.broadcast_to((pooled[g] * scale)[m : m + 1, :], (16, L)).astype(BF16)
+            for g in range(NY)
+            for m in range(M)
+        ],
+        axis=1,
+    )
+    classifier = table[...].reshape(TILES * L, L)
+    logits = jnp.dot(wide, classifier, preferred_element_type=F32)
+    logits_ref[...] = logits[0:1, :]
 
     stores = []
 
@@ -375,45 +471,8 @@
             store.start()
             stores.append(store)
 
-    def sum_plane():
-        for copy in pool_copies:
-            copy.wait_recv()
-        total = pool_plane[0]
-        for q in range(1, NY * NC):
-            total = total + pool_plane[q]
-        pool_sum[...] = total
-        pool_axis[z] = total
-        return [
-            push(pool_sum, pool_axis.at[z], small_s.at[18 + k], small_r.at[18 + k], to_z[k])
-            for k in FAR_Z
-        ]
-
-    if NCH == 1:
-        last_copies = sum_plane()
-        final(0)
-    else:
-        final(0)
-        last_copies = sum_plane()
-        for i in range(1, NCH):
-            final(i)
-
-    for copy in table_copies:
-        copy.wait_recv()
-    loads[3].wait()
-    for copy in last_copies:
-        copy.wait_recv()
-    pooled = pool_axis[0]
-    for q in range(1, NZ):
-        pooled = pooled + pool_axis[q]
-    pooled = pooled / (G * NZ * NY * NC)
-    square = jnp.sum(pooled * pooled, keepdims=True) / (TILES * L)
-    normed = (pooled / jnp.sqrt(square + EPS)).astype(BF16)
-    wide = jnp.concatenate(
-        [jnp.broadcast_to(normed[j : j + 1, :], (16, L)) for j in range(TILES)], axis=1
-    )
-    classifier = table[...].reshape(TILES * L, L)
-    logits = jnp.dot(wide, classifier, preferred_element_type=F32)
-    logits_ref[...] = logits[0:1, :]
+    for i in range(NCH):
+        final(i)
 
     for store in stores:
         store.wait()
@@ -456,8 +515,6 @@
         pltpu.VMEM((NY, 8, L), F32),
         pltpu.VMEM((NY, 8, L), F32),
         pltpu.VMEM((NY, 8, L), F32),
-        pltpu.VMEM((8, L), F32),
-        pltpu.VMEM((NZ, 8, L), F32),
         pltpu.VMEM((NY, M * 8, L), F32),
         pltpu.VMEM((NY, M * 8, L), F32),
         pltpu.VMEM((NY, M * 8, L), F32),
@@ -465,16 +522,21 @@
         pltpu.VMEM((NZ, M * 8, L), F32),
         pltpu.VMEM((2, HEADS, L), F32),
         pltpu.VMEM((2, HEADS, L), F32),
-        pltpu.VMEM((32, L), F32),
-        pltpu.VMEM((32, L), F32),
-        pltpu.VMEM((NY * NC, 32, L), F32),
-        pltpu.VMEM((32, L), F32),
-        pltpu.VMEM((NZ, 32, L), F32),
+        pltpu.VMEM((NY, 2, 16, L), F32),
+        pltpu.VMEM((NY, 2, 16, L), F32),
+        pltpu.VMEM((24, L), F32),
+        pltpu.VMEM((NZ, 24, L), F32),
+        pltpu.VMEM((NY, 8, L), F32),
+        pltpu.VMEM((NY, 8, L), F32),
+        pltpu.VMEM((8, L), F32),
+        pltpu.VMEM((NZ, 8, L), F32),
+        pltpu.VMEM((8, L), F32),
+        pltpu.VMEM((NY * NC, 8, L), F32),
         *[ref for _, count in CHUNKS for ref in chunk(count)],
         dma((4,)), dma((NCH * NY,)),
         dma((2 * NCH,)), dma((2 * NCH,)), dma((NCH, 7)), dma((NCH, 7)),
         dma((NCH, NZ)), dma((NCH, NZ)), dma((NCH, NZ)), dma((NCH, NZ)),
-        dma((NX,)), dma((NX,)), dma((26,)), dma((26,)),
+        dma((NX,)), dma((NX,)), dma((32,)), dma((32,)),
     ]
     mixed, logits = pl.pallas_call(
         kernel,

time: 48.2 us -> 45.4 us (0.942)
  Pallas kernels: 44.8 us -> 41.9 us
    pallas_call x1, Pallas kernels: 44.8 us -> 41.9 us  [local(): pl.pallas_call(kernel, out_shape=(jax.ShapeDtypeStruct((positions, channe...]
where the time goes in v3:
time: 45.4 us; the launch traced here: 45.3 us
  Pallas kernels  41.9 us (92%)
  local copies, waits for them, and re-layouts  2.68 us (6%)
  between operations  0.65 us (1%)
    pallas_call x1, Pallas kernels, local(): pl.pallas_call(kernel, out_shape=(jax.ShapeDtypeStruct((positions, channe...  41.9 us
    unnamed x4, local copies, waits for them, and re-layouts  2.68 us

profile of v3, /device:TPU:1, one launch (start us, length us, event | category | flops | bytes accessed | tf_op | source)
XLA Modules:
  0.0 45.3 jit_solution(13451281613440055020)
XLA Ops:
  0.6 41.9 %shard_map.68 = (bf16[128,3584]{1,0:T(8,128)(2,1)}, f32[1,128]{1,0:T(1,128)}) custom-call(bf16[128,3584]{1,0:T(8,128)(2,1)} %bitcast.5, bf16[128,256]{1,0:T(8,128)(2,1)} %bitcast.6, f32[56,128]{1,0:T(8,128)} %bitcast.7, f32[56]{0:T(128)} %skip_ref.1, bf16[896,128]{1,0:T(8,128)(2,1)} %cls_ref.1), custom_call_target="tpu_custom_call" | custom-call | tf_op jit(solution)/shard_map/pallas_call | solution.py:541
  42.6 0.0 copy-start
  42.6 2.2 %copy.9 = bf16[1,128,3584]{2,1,0:T(8,128)(2,1)} copy(bf16[1,128,3584]{2,1,0:T(8,128)(2,1)} %bitcast.4) | data formatting | bytes 1835008
  44.7 0.0 copy-done
  44.7 0.5 %copy.10 = f32[1,128]{1,0:T(1,128)} copy(f32[1,128]{1,0:T(1,128)S(1)} %copy-done) | data formatting | bytes 1024
Async XLA Ops:
  42.6 2.2 %copy-start = (f32[1,128]{1,0:T(1,128)S(1)}, f32[1,128]{1,0:T(1,128)}, u32[]{:S(2)}) copy-start(f32[1,128]{1,0:T(1,128)} %get-tuple-element.9) | copy-start | bytes 1540

commit v4 on v3

--- a/solution.py
+++ b/solution.py
@@ -19,6 +19,7 @@
 CHUNKS = ((0, 4), (4, 3))
 NCH = len(CHUNKS)
 EPS = 1e-06
+PIECES = 8
 FAR_Y = (2, 1, 3)
 FAR_Z = (4, 5, 3, 6, 2, 7, 1)
 
@@ -33,14 +34,14 @@
     v_hbm, kq_hbm, ld_hbm, skip_ref, cls_ref, mixed_ref, logits_ref,
     v_ref, kq_ref, ld_ref, out_ref, grow, local_out, table,
     decay_own, decay_pair, decay_chip, decay_plane,
-    pair_factor, start_factor, plane_factor, plane_start, axis_factor,
+    pair_factor, start_factor, plane_factor, plane_start,
     response, response_pair, chip_response, plane_response, axis_note, axis_notes,
     pool_own, pool_parts, pool_send, pool_axis, pool_sum, pool_plane,
     *rest,
 ):
     buffers = [rest[i * 12 : (i + 1) * 12] for i in range(NCH)]
     (in_s, out_s, pair_s, pair_r, plane_s, plane_r, axis_s, axis_r,
-     back_s, back_r, table_s, table_r, small_s, small_r) = rest[NCH * 12 :]
+     back_s, back_r, note_s, note_r, table_s, table_r, small_s, small_r) = rest[NCH * 12 :]
     me, x = lax.axis_index("seq"), lax.axis_index("fsdp")
     c = lax.rem(me, NC)
     y = lax.rem(me // NC, NY)
@@ -96,9 +97,6 @@
     causal = row >= col
     lower = jnp.where(causal, 1.0, 0.0).astype(F32)
     log_decay = ld_ref[...]
-    cum = lax.dot_general(
-        log_decay, lower, (((1,), (1,)), ((), ())), precision=HIGHEST, preferred_element_type=F32
-    )
     cum_t = lax.dot_general(
         lower, log_decay, (((1,), (1,)), ((), ())), precision=HIGHEST, preferred_element_type=F32
     )
@@ -189,6 +187,9 @@
     table_copies = [
         push(cls_ref, table.at[x], table_s.at[k], table_r.at[k], to_x[k]) for k in range(1, NX)
     ]
+    cum = lax.dot_general(
+        log_decay, lower, (((1,), (1,)), ((), ())), precision=HIGHEST, preferred_element_type=F32
+    )
     inside(0)
 
     pair_decay.wait_recv()
@@ -255,10 +256,8 @@
     axis_note[8:24, :] = summed
     axis_notes[z, 0:8, :] = run
     axis_notes[z, 8:24, :] = summed
-    note_copies = [
-        push(axis_note, axis_notes.at[z], small_s.at[7 + k], small_r.at[7 + k], to_z[k])
-        for k in FAR_Z
-    ]
+    for k in FAR_Z:
+        push(axis_note, axis_notes.at[z], note_s.at[k], note_r.at[z], to_z[k])
     inside(2)
     inside(3)
     mine_1 = jnp.where(c == 0, resp_1, pltpu.roll(resp_1, 64, 1))
@@ -295,7 +294,7 @@
             else:
                 axis_send[k] = total.astype(BF16)
                 axis_copies[i].append(
-                    push(axis_send.at[k], axis_recv.at[z], axis_s.at[i, k], axis_r.at[i, k], to_z[k])
+                    push(axis_send.at[k], axis_recv.at[z], axis_s.at[i, k], axis_r.at[i, z], to_z[k])
                 )
     for copy in part_copies:
         copy.wait_recv()
@@ -318,34 +317,78 @@
                 first, count,
             )
         )
-    for copy in note_copies:
-        copy.wait_recv()
+    half_queries = jnp.where(
+        c == 0, queries.astype(F32), pltpu.roll(queries.astype(F32), 64, 1)
+    ).astype(BF16)
+
+    def from_z(q):
+        note = pltpu.make_async_remote_copy(
+            src_ref=axis_note, dst_ref=axis_notes.at[q], send_sem=note_s.at[0], recv_sem=note_r.at[q],
+            device_id=at(q, y, c), device_id_type=MESH,
+        )
+        return [note] + [
+            pltpu.make_async_remote_copy(
+                src_ref=buffers[i][4].at[0], dst_ref=buffers[i][5].at[q],
+                send_sem=axis_s.at[i, 0], recv_sem=axis_r.at[i, q],
+                device_id=at(q, y, c), device_id_type=MESH,
+            )
+            for i in range(NCH)
+        ]
+
+    def back(q):
+        return [
+            pltpu.make_async_remote_copy(
+                src_ref=buffers[i][6].at[q], dst_ref=buffers[i][7].at[z],
+                send_sem=back_s.at[i, q], recv_sem=back_r.at[i, z],
+                device_id=at(q, y, c), device_id_type=MESH,
+            )
+            for i in range(NCH)
+        ]
+
+    def from_back(q, i):
+        return pltpu.make_async_remote_copy(
+            src_ref=buffers[i][6].at[0], dst_ref=buffers[i][7].at[q],
+            send_sem=back_s.at[i, 0], recv_sem=back_r.at[i, q],
+            device_id=at(q, y, c), device_id_type=MESH,
+        )
+
+    totals = [jnp.zeros((count * 8, L), F32) for _, count in CHUNKS]
+    for q in range(NZ):
+        for i in range(NCH):
+            buffers[i][6][q] = totals[i].astype(BF16)
+        if q > 0:
+
+            @pl.when(z != q)
+            def _(q=q):
+                for copy in back(q):
+                    copy.start()
+
+            @pl.when(z == q)
+            def _(q=q):
+                for i in range(NCH):
+                    buffers[i][7][q] = buffers[i][6][q]
+
+        @pl.when(z != q)
+        def _(q=q):
+            for copy in from_z(q):
+                copy.wait_recv()
+
+        if q < NZ - 1:
+            factor = spread(jnp.exp(axis_notes[q, 0:8, :]))
+            for i, (first, count) in enumerate(CHUNKS):
+                rows = slice(first * 8, (first + count) * 8)
+                totals[i] = factor[rows, :] * totals[i] + buffers[i][5][q].astype(F32)
+
+    @pl.when(z == 0)
+    def _():
+        for i in range(NCH):
+            buffers[i][7][...] = jnp.zeros_like(buffers[i][7])
+
     lane = lax.broadcasted_iota(jnp.int32, (16, L), 1) // 8
     my_rows = jnp.zeros((16, L), F32)
     for q in range(NZ):
-        axis_factor[q] = spread(jnp.exp(axis_notes[q, 0:8, :]))
         turned = pltpu.roll(axis_notes[q, 8:24, :], lax.rem(2 * L + 8 * q - 64 * c - 8 * z, L), 1)
         my_rows = my_rows + jnp.where(lane == q, turned, 0.0)
-    half_queries = jnp.where(
-        c == 0, queries.astype(F32), pltpu.roll(queries.astype(F32), 64, 1)
-    ).astype(BF16)
-
-    back_copies = [[] for _ in CHUNKS]
-    for i, (first, count) in enumerate(CHUNKS):
-        axis_recv, axis_prefix, start_plane = buffers[i][5:8]
-        rows = slice(first * 8, (first + count) * 8)
-        for copy in axis_copies[i]:
-            copy.wait_recv()
-        total = jnp.zeros((count * 8, L), F32)
-        for q in range(NZ):
-            axis_prefix[q] = total.astype(BF16)
-            if q < NZ - 1:
-                total = axis_factor[q, rows, :] * total + axis_recv[q].astype(F32)
-        back_copies[i] = [
-            push(axis_prefix.at[zs[k]], start_plane.at[z], back_s.at[i, k], back_r.at[i, k], to_z[k])
-            for k in FAR_Z
-        ]
-        start_plane[z] = axis_prefix[z]
     for i, (first, count) in enumerate(CHUNKS):
         axis_prefix = buffers[i][6]
         pool_tiles[i] = pool_tiles[i] + pool_rows(
@@ -364,13 +407,19 @@
         for k in FAR_Z
     ]
 
+    earlier = list(sends)
+    sends.clear()
     chip_copies = [[] for _ in CHUNKS]
     for i, (first, count) in enumerate(CHUNKS):
         plane_prefix = buffers[i][3]
         start_plane, start_send, start_chip = buffers[i][7:10]
         rows = slice(first * 8, (first + count) * 8)
-        for copy in back_copies[i]:
-            copy.wait_recv()
+        for q in range(NZ):
+
+            @pl.when((z != q) & (z > 0))
+            def _(q=q, i=i):
+                from_back(q, i).wait_recv()
+
         for k in (*FAR_Y, 0):
             g = ys[k]
 
@@ -386,6 +435,30 @@
                 chip_copies[i].append(
                     push(start_send.at[k], start_chip.at[y], plane_s.at[i, 3 + k], plane_r.at[i, 3 + k], to_y[k])
                 )
+
+    for copy in earlier:
+        copy.wait_send()
+
+    half_copies = []
+    for i, (first, count) in enumerate(CHUNKS):
+        state = buffers[i][0]
+        start_chip, carried, carried_recv = buffers[i][9:12]
+        rows = slice(first * 8, (first + count) * 8)
+        for copy in chip_copies[i]:
+            copy.wait_recv()
+
+        @pl.loop(0, NY)
+        def _(g):
+            @pl.loop(0, NZ)
+            def _(b):
+                before = start_chip[g, b].astype(F32)
+                after = start_factor[g, rows, :] * before + state[0, g, b].astype(F32)
+                carried[0, g, b] = start_chip[g, b]
+                carried[1, g, b] = after.astype(BF16)
+
+        half_copies.append(
+            push(carried.at[other], carried_recv, pair_s.at[NCH + i], pair_r.at[NCH + i], to_pair)
+        )
 
     for copy in pool_copies:
         copy.wait_recv()
@@ -400,49 +473,6 @@
         + [push(pool_sum, mine, small_s.at[27 + k], small_r.at[27 + k], to_y_other[k]) for k in FAR_Y]
         + [push(pool_sum, mine, small_s.at[31], small_r.at[31], to_pair)]
     )
-
-    half_copies = []
-    for i, (first, count) in enumerate(CHUNKS):
-        state = buffers[i][0]
-        start_chip, carried, carried_recv = buffers[i][9:12]
-        rows = slice(first * 8, (first + count) * 8)
-        for copy in chip_copies[i]:
-            copy.wait_recv()
-
-        @pl.loop(0, NY)
-        def _(g):
-            @pl.loop(0, NZ)
-            def _(b):
-                before = start_chip[g, b].astype(F32)
-                after = start_factor[g, rows, :] * before + state[0, g, b].astype(F32)
-                carried[0, g, b] = start_chip[g, b]
-                carried[1, g, b] = after.astype(BF16)
-
-        half_copies.append(
-            push(carried.at[other], carried_recv, pair_s.at[NCH + i], pair_r.at[NCH + i], to_pair)
-        )
-
-    for copy in table_copies:
-        copy.wait_recv()
-    loads[3].wait()
-    for copy in last_copies:
-        copy.wait_recv()
-    pooled = [
-        (pool_plane[NC * g] + pool_plane[NC * g + 1]) / (G * NZ * NY * NC) for g in range(NY)
-    ]
-    square = sum(jnp.sum(p * p, keepdims=True) for p in pooled) / (TILES * L)
-    scale = 1.0 / jnp.sqrt(square + EPS)
-    wide = jnp.concatenate(
-        [
-            jnp.broadcast_to((pooled[g] * scale)[m : m + 1, :], (16, L)).astype(BF16)
-            for g in range(NY)
-            for m in range(M)
-        ],
-        axis=1,
-    )
-    classifier = table[...].reshape(TILES * L, L)
-    logits = jnp.dot(wide, classifier, preferred_element_type=F32)
-    logits_ref[...] = logits[0:1, :]
 
     stores = []
 
@@ -474,10 +504,55 @@
     for i in range(NCH):
         final(i)
 
+    for copy in table_copies:
+        copy.wait_recv()
+    loads[3].wait()
+    for copy in last_copies:
+        copy.wait_recv()
+    pooled = [
+        (pool_plane[NC * g] + pool_plane[NC * g + 1]) / (G * NZ * NY * NC) for g in range(NY)
+    ]
+    square = sum(jnp.sum(p * p, keepdims=True) for p in pooled) / (TILES * L)
+    scale = 1.0 / jnp.sqrt(square + EPS)
+    wide = jnp.concatenate(
+        [
+            jnp.broadcast_to((pooled[g] * scale)[m : m + 1, :], (16, L)).astype(BF16)
+            for g in range(NY)
+            for m in range(M)
+        ],
+        axis=1,
+    )
+    classifier = table[...].reshape(TILES * L, L)
+    logits = jnp.dot(wide, classifier, preferred_element_type=F32)
+    logits_ref[...] = logits[0:1, :]
+
     for store in stores:
         store.wait()
+    for q in range(1, NZ):
+
+        @pl.when(z != q)
+        def _(q=q):
+            for copy in back(q):
+                copy.wait_send()
+
     for copy in sends:
         copy.wait_send()
+
+
+def hand_over(mixed_in, logits_in, mixed_out, logits_out, mixed, logits, in_sem, out_sem):
+    pairs = [(logits_in, logits, logits_out)]
+    for i in range(PIECES):
+        rows = slice(i * (G // PIECES), (i + 1) * (G // PIECES))
+        pairs.append((mixed_in.at[rows, :], mixed.at[rows, :], mixed_out.at[rows, :]))
+    loads = [pltpu.make_async_copy(a, b, in_sem.at[i]) for i, (a, b, _) in enumerate(pairs)]
+    stores = [pltpu.make_async_copy(b, c, out_sem.at[i]) for i, (_, b, c) in enumerate(pairs)]
+    for load in loads:
+        load.start()
+    for load, store in zip(loads, stores):
+        load.wait()
+        store.start()
+    for store in stores:
+        store.wait()
 
 
 def local(inputs, keys_queries, log_decay, skip, classifier):
@@ -519,7 +594,6 @@
         pltpu.VMEM((NY, M * 8, L), F32),
         pltpu.VMEM((NY, M * 8, L), F32),
         pltpu.VMEM((NY, M * 8, L), F32),
-        pltpu.VMEM((NZ, M * 8, L), F32),
         pltpu.VMEM((2, HEADS, L), F32),
         pltpu.VMEM((2, HEADS, L), F32),
         pltpu.VMEM((NY, 2, 16, L), F32),
@@ -536,7 +610,7 @@
         dma((4,)), dma((NCH * NY,)),
         dma((2 * NCH,)), dma((2 * NCH,)), dma((NCH, 7)), dma((NCH, 7)),
         dma((NCH, NZ)), dma((NCH, NZ)), dma((NCH, NZ)), dma((NCH, NZ)),
-        dma((NX,)), dma((NX,)), dma((32,)), dma((32,)),
+        dma((NZ,)), dma((NZ,)), dma((NX,)), dma((NX,)), dma((32,)), dma((32,)),
     ]
     mixed, logits = pl.pallas_call(
         kernel,
@@ -557,6 +631,22 @@
         skip,
         classifier,
     )
+    mixed, logits = pl.pallas_call(
+        hand_over,
+        out_shape=(
+            jax.ShapeDtypeStruct(mixed.shape, mixed.dtype),
+            jax.ShapeDtypeStruct(logits.shape, logits.dtype),
+        ),
+        in_specs=[hbm, hbm],
+        out_specs=(hbm, hbm),
+        scratch_shapes=[
+            pltpu.VMEM(mixed.shape, mixed.dtype),
+            pltpu.VMEM(logits.shape, logits.dtype),
+            dma((PIECES + 1,)),
+            dma((PIECES + 1,)),
+        ],
+        compiler_params=pltpu.CompilerParams(vmem_limit_bytes=60 << 20),
+    )(mixed, logits)
     return mixed.reshape(copies, positions, channels), logits
 
 

time: 45.4 us -> 45.4 us (level)
  the two profiles are of different devices: /device:TPU:1 before, /device:TPU:39 now
where the time goes in v4:
time: 45.4 us; the launch traced here: 45.3 us
  Pallas kernels  44.6 us (98%)
  between operations  0.64 us (1%)
    pallas_call x1, Pallas kernels, local(): pl.pallas_call(kernel, out_shape=(jax.ShapeDtypeStruct((positions, channe...  42.6 us
    pallas_call x1, Pallas kernels, local(): pl.pallas_call(hand_over, out_shape=(jax.ShapeDtypeStruct(mixed.shape, mi...  2.06 us

profile of v4, /device:TPU:39, one launch (start us, length us, event | category | flops | bytes accessed | tf_op | source)
XLA Modules:
  0.0 45.3 jit_solution(1102418476452935673)
XLA Ops:
  0.6 42.6 %shard_map.68 = (bf16[128,3584]{1,0:T(8,128)(2,1)}, f32[1,128]{1,0:T(1,128)}) custom-call(bf16[128,3584]{1,0:T(8,128)(2,1)} %bitcast.4, bf16[128,256]{1,0:T(8,128)(2,1)} %bitcast.5, f32[56,128]{1,0:T(8,128)} %bitcast.6, f32[56]{0:T(128)} %skip_ref.1, bf16[896,128]{1,0:T(8,128)(2,1)} %cls_ref.1), custom_call_target="tpu_custom_call" | custom-call | tf_op jit(solution)/shard_map/pallas_call | solution.py:615
  43.2 2.1 %shard_map.69 = (bf16[128,3584]{1,0:T(8,128)(2,1)}, f32[1,128]{1,0:T(1,128)}) custom-call(bf16[128,3584]{1,0:T(8,128)(2,1)} %get-tuple-element.6.mixed_in, f32[1,128]{1,0:T(1,128)} %get-tuple-element.7.logits_in), custom_call_target="tpu_custom_call" | custom-call | tf_op jit(solution)/shard_map/pallas_call | solution.py:634

commit v5 on v4

--- a/solution.py
+++ b/solution.py
@@ -439,27 +439,6 @@
     for copy in earlier:
         copy.wait_send()
 
-    half_copies = []
-    for i, (first, count) in enumerate(CHUNKS):
-        state = buffers[i][0]
-        start_chip, carried, carried_recv = buffers[i][9:12]
-        rows = slice(first * 8, (first + count) * 8)
-        for copy in chip_copies[i]:
-            copy.wait_recv()
-
-        @pl.loop(0, NY)
-        def _(g):
-            @pl.loop(0, NZ)
-            def _(b):
-                before = start_chip[g, b].astype(F32)
-                after = start_factor[g, rows, :] * before + state[0, g, b].astype(F32)
-                carried[0, g, b] = start_chip[g, b]
-                carried[1, g, b] = after.astype(BF16)
-
-        half_copies.append(
-            push(carried.at[other], carried_recv, pair_s.at[NCH + i], pair_r.at[NCH + i], to_pair)
-        )
-
     for copy in pool_copies:
         copy.wait_recv()
     total = pool_axis[0]
@@ -473,6 +452,27 @@
         + [push(pool_sum, mine, small_s.at[27 + k], small_r.at[27 + k], to_y_other[k]) for k in FAR_Y]
         + [push(pool_sum, mine, small_s.at[31], small_r.at[31], to_pair)]
     )
+
+    half_copies = []
+    for i, (first, count) in enumerate(CHUNKS):
+        state = buffers[i][0]
+        start_chip, carried, carried_recv = buffers[i][9:12]
+        rows = slice(first * 8, (first + count) * 8)
+        for copy in chip_copies[i]:
+            copy.wait_recv()
+
+        @pl.loop(0, NY)
+        def _(g):
+            @pl.loop(0, NZ)
+            def _(b):
+                before = start_chip[g, b].astype(F32)
+                after = start_factor[g, rows, :] * before + state[0, g, b].astype(F32)
+                carried[0, g, b] = start_chip[g, b]
+                carried[1, g, b] = after.astype(BF16)
+
+        half_copies.append(
+            push(carried.at[other], carried_recv, pair_s.at[NCH + i], pair_r.at[NCH + i], to_pair)
+        )
 
     stores = []
 

time: 45.4 us -> 43.4 us (0.956)
  Pallas kernels: 44.6 us -> 42.6 us
    pallas_call x1, Pallas kernels: 42.6 us -> 40.5 us  [local(): pl.pallas_call(kernel, out_shape=(jax.ShapeDtypeStruct((positions, channe...]
where the time goes in v5:
time: 43.4 us; the launch traced here: 43.2 us
  Pallas kernels  42.6 us (98%)
  between operations  0.64 us (1%)
    pallas_call x1, Pallas kernels, local(): pl.pallas_call(kernel, out_shape=(jax.ShapeDtypeStruct((positions, channe...  40.5 us
    pallas_call x1, Pallas kernels, local(): pl.pallas_call(hand_over, out_shape=(jax.ShapeDtypeStruct(mixed.shape, mi...  2.06 us

profile of v5, /device:TPU:39, one launch (start us, length us, event | category | flops | bytes accessed | tf_op | source)
XLA Modules:
  0.0 43.2 jit_solution(16160855289134609482)
XLA Ops:
  0.6 40.5 %shard_map.68 = (bf16[128,3584]{1,0:T(8,128)(2,1)}, f32[1,128]{1,0:T(1,128)}) custom-call(bf16[128,3584]{1,0:T(8,128)(2,1)} %bitcast.4, bf16[128,256]{1,0:T(8,128)(2,1)} %bitcast.5, f32[56,128]{1,0:T(8,128)} %bitcast.6, f32[56]{0:T(128)} %skip_ref.1, bf16[896,128]{1,0:T(8,128)(2,1)} %cls_ref.1), custom_call_target="tpu_custom_call" | custom-call | tf_op jit(solution)/shard_map/pallas_call | solution.py:615
  41.2 2.1 %shard_map.69 = (bf16[128,3584]{1,0:T(8,128)(2,1)}, f32[1,128]{1,0:T(1,128)}) custom-call(bf16[128,3584]{1,0:T(8,128)(2,1)} %get-tuple-element.6.mixed_in, f32[1,128]{1,0:T(1,128)} %get-tuple-element.7.logits_in), custom_call_target="tpu_custom_call" | custom-call | tf_op jit(solution)/shard_map/pallas_call | solution.py:634

commit v6 on v5

--- a/solution.py
+++ b/solution.py
@@ -296,6 +296,73 @@
                 axis_copies[i].append(
                     push(axis_send.at[k], axis_recv.at[z], axis_s.at[i, k], axis_r.at[i, z], to_z[k])
                 )
+    half_queries = jnp.where(
+        c == 0, queries.astype(F32), pltpu.roll(queries.astype(F32), 64, 1)
+    ).astype(BF16)
+
+    def from_z(q):
+        note = pltpu.make_async_remote_copy(
+            src_ref=axis_note, dst_ref=axis_notes.at[q], send_sem=note_s.at[0], recv_sem=note_r.at[q],
+            device_id=at(q, y, c), device_id_type=MESH,
+        )
+        return [note] + [
+            pltpu.make_async_remote_copy(
+                src_ref=buffers[i][4].at[0], dst_ref=buffers[i][5].at[q],
+                send_sem=axis_s.at[i, 0], recv_sem=axis_r.at[i, q],
+                device_id=at(q, y, c), device_id_type=MESH,
+            )
+            for i in range(NCH)
+        ]
+
+    def back(q):
+        return [
+            pltpu.make_async_remote_copy(
+                src_ref=buffers[i][6].at[q], dst_ref=buffers[i][7].at[z],
+                send_sem=back_s.at[i, q], recv_sem=back_r.at[i, z],
+                device_id=at(q, y, c), device_id_type=MESH,
+            )
+            for i in range(NCH)
+        ]
+
+    def from_back(q, i):
+        return pltpu.make_async_remote_copy(
+            src_ref=buffers[i][6].at[0], dst_ref=buffers[i][7].at[q],
+            send_sem=back_s.at[i, 0], recv_sem=back_r.at[i, q],
+            device_id=at(q, y, c), device_id_type=MESH,
+        )
+
+    totals = [jnp.zeros((count * 8, L), F32) for _, count in CHUNKS]
+    for q in range(NZ):
+        for i in range(NCH):
+            buffers[i][6][q] = totals[i].astype(BF16)
+        if q > 0:
+
+            @pl.when(z != q)
+            def _(q=q):
+                for copy in back(q):
+                    copy.start()
+
+            @pl.when(z == q)
+            def _(q=q):
+                for i in range(NCH):
+                    buffers[i][7][q] = buffers[i][6][q]
+
+        @pl.when(z != q)
+        def _(q=q):
+            for copy in from_z(q):
+                copy.wait_recv()
+
+        if q < NZ - 1:
+            factor = spread(jnp.exp(axis_notes[q, 0:8, :]))
+            for i, (first, count) in enumerate(CHUNKS):
+                rows = slice(first * 8, (first + count) * 8)
+                totals[i] = factor[rows, :] * totals[i] + buffers[i][5][q].astype(F32)
+
+    @pl.when(z == 0)
+    def _():
+        for i in range(NCH):
+            buffers[i][7][...] = jnp.zeros_like(buffers[i][7])
+
     for copy in part_copies:
         copy.wait_recv()
     my_half = [
@@ -317,73 +384,6 @@
                 first, count,
             )
         )
-    half_queries = jnp.where(
-        c == 0, queries.astype(F32), pltpu.roll(queries.astype(F32), 64, 1)
-    ).astype(BF16)
-
-    def from_z(q):
-        note = pltpu.make_async_remote_copy(
-            src_ref=axis_note, dst_ref=axis_notes.at[q], send_sem=note_s.at[0], recv_sem=note_r.at[q],
-            device_id=at(q, y, c), device_id_type=MESH,
-        )
-        return [note] + [
-            pltpu.make_async_remote_copy(
-                src_ref=buffers[i][4].at[0], dst_ref=buffers[i][5].at[q],
-                send_sem=axis_s.at[i, 0], recv_sem=axis_r.at[i, q],
-                device_id=at(q, y, c), device_id_type=MESH,
-            )
-            for i in range(NCH)
-        ]
-
-    def back(q):
-        return [
-            pltpu.make_async_remote_copy(
-                src_ref=buffers[i][6].at[q], dst_ref=buffers[i][7].at[z],
-                send_sem=back_s.at[i, q], recv_sem=back_r.at[i, z],
-                device_id=at(q, y, c), device_id_type=MESH,
-            )
-            for i in range(NCH)
-        ]
-
-    def from_back(q, i):
-        return pltpu.make_async_remote_copy(
-            src_ref=buffers[i][6].at[0], dst_ref=buffers[i][7].at[q],
-            send_sem=back_s.at[i, 0], recv_sem=back_r.at[i, q],
-            device_id=at(q, y, c), device_id_type=MESH,
-        )
-
-    totals = [jnp.zeros((count * 8, L), F32) for _, count in CHUNKS]
-    for q in range(NZ):
-        for i in range(NCH):
-            buffers[i][6][q] = totals[i].astype(BF16)
-        if q > 0:
-
-            @pl.when(z != q)
-            def _(q=q):
-                for copy in back(q):
-                    copy.start()
-
-            @pl.when(z == q)
-            def _(q=q):
-                for i in range(NCH):
-                    buffers[i][7][q] = buffers[i][6][q]
-
-        @pl.when(z != q)
-        def _(q=q):
-            for copy in from_z(q):
-                copy.wait_recv()
-
-        if q < NZ - 1:
-            factor = spread(jnp.exp(axis_notes[q, 0:8, :]))
-            for i, (first, count) in enumerate(CHUNKS):
-                rows = slice(first * 8, (first + count) * 8)
-                totals[i] = factor[rows, :] * totals[i] + buffers[i][5][q].astype(F32)
-
-    @pl.when(z == 0)
-    def _():
-        for i in range(NCH):
-            buffers[i][7][...] = jnp.zeros_like(buffers[i][7])
-
     lane = lax.broadcasted_iota(jnp.int32, (16, L), 1) // 8
     my_rows = jnp.zeros((16, L), F32)
     for q in range(NZ):

time: 43.4 us -> 43.5 us (level)
  no operation moved by 1% of the time
where the time goes in v6:
time: 43.5 us; the launch traced here: 43.4 us
  Pallas kernels  42.7 us (98%)
  between operations  0.64 us (1%)
    pallas_call x1, Pallas kernels, local(): pl.pallas_call(kernel, out_shape=(jax.ShapeDtypeStruct((positions, channe...  40.7 us
    pallas_call x1, Pallas kernels, local(): pl.pallas_call(hand_over, out_shape=(jax.ShapeDtypeStruct(mixed.shape, mi...  2.06 us

profile of v6, /device:TPU:39, one launch (start us, length us, event | category | flops | bytes accessed | tf_op | source)
XLA Modules:
  0.0 43.4 jit_solution(17889493862749819687)
XLA Ops:
  0.6 40.7 %shard_map.68 = (bf16[128,3584]{1,0:T(8,128)(2,1)}, f32[1,128]{1,0:T(1,128)}) custom-call(bf16[128,3584]{1,0:T(8,128)(2,1)} %bitcast.4, bf16[128,256]{1,0:T(8,128)(2,1)} %bitcast.5, f32[56,128]{1,0:T(8,128)} %bitcast.6, f32[56]{0:T(128)} %skip_ref.1, bf16[896,128]{1,0:T(8,128)(2,1)} %cls_ref.1), custom_call_target="tpu_custom_call" | custom-call | tf_op jit(solution)/shard_map/pallas_call | solution.py:615
  41.3 2.1 %shard_map.69 = (bf16[128,3584]{1,0:T(8,128)(2,1)}, f32[1,128]{1,0:T(1,128)}) custom-call(bf16[128,3584]{1,0:T(8,128)(2,1)} %get-tuple-element.6.mixed_in, f32[1,128]{1,0:T(1,128)} %get-tuple-element.7.logits_in), custom_call_target="tpu_custom_call" | custom-call | tf_op jit(solution)/shard_map/pallas_call | solution.py:634

commit v7 on v6

--- a/solution.py
+++ b/solution.py
@@ -67,10 +67,19 @@
     loads = [
         pltpu.make_async_copy(src, dst, in_s.at[i])
         for i, (src, dst) in enumerate(
-            ((ld_hbm, ld_ref), (kq_hbm, kq_ref), (v_hbm, v_ref), (cls_ref, table.at[x]))
-        )
-    ]
-    for load in loads:
+            ((ld_hbm, ld_ref), (kq_hbm, kq_ref), (cls_ref, table.at[x]))
+        )
+    ]
+    value_loads = []
+    for i, (first, count) in enumerate(CHUNKS):
+        for g in range(NY):
+            lanes = slice((g * M + first) * L, (g * M + first + count) * L)
+            value_loads.append(
+                pltpu.make_async_copy(
+                    v_hbm.at[:, lanes], v_ref.at[:, lanes], in_s.at[3 + i * NY + g]
+                )
+            )
+    for load in (*loads[:2], *value_loads, loads[2]):
         load.start()
 
     sends = []
@@ -95,16 +104,20 @@
     row = lax.broadcasted_iota(jnp.int32, (G, G), 0)
     col = lax.broadcasted_iota(jnp.int32, (G, G), 1)
     causal = row >= col
-    lower = jnp.where(causal, 1.0, 0.0).astype(F32)
     log_decay = ld_ref[...]
+    high = log_decay.astype(BF16)
+    middle = (log_decay - high.astype(F32)).astype(BF16)
+    low = (log_decay - high.astype(F32) - middle.astype(F32)).astype(BF16)
+    decay_parts = jnp.concatenate([high, middle, low], axis=1)
+    lower = jnp.where(causal, 1.0, 0.0).astype(BF16)
+    lower = jnp.concatenate([lower] * 3, axis=1)
     cum_t = lax.dot_general(
-        lower, log_decay, (((1,), (1,)), ((), ())), precision=HIGHEST, preferred_element_type=F32
+        lower, decay_parts, (((1,), (1,)), ((), ())), preferred_element_type=F32
     )
     loads[1].wait()
     keys = kq_ref[:, :N]
     queries = kq_ref[:, N:]
     keys_t = keys.T
-    loads[2].wait()
 
     def pool_rows(responses, parts, first, count):
         whole = jnp.concatenate(responses, axis=1)
@@ -123,6 +136,7 @@
         first, count = CHUNKS[i]
         state = buffers[i][0]
         for g in range(NY):
+            value_loads[i * NY + g].wait()
             for m in range(count):
                 j = g * M + first + m
                 lanes = slice(j * L, (j + 1) * L)
@@ -188,7 +202,7 @@
         push(cls_ref, table.at[x], table_s.at[k], table_r.at[k], to_x[k]) for k in range(1, NX)
     ]
     cum = lax.dot_general(
-        log_decay, lower, (((1,), (1,)), ((), ())), precision=HIGHEST, preferred_element_type=F32
+        decay_parts, lower, (((1,), (1,)), ((), ())), preferred_element_type=F32
     )
     inside(0)
 
@@ -212,7 +226,7 @@
         for k in (*FAR_Y, 0):
             g = ys[k]
 
-            @pl.loop(0, NZ)
+            @pl.loop(0, NZ, unroll=True)
             def _(b, g=g, k=k):
                 total = pair_factor[g, rows, :] * state[0, g, b].astype(F32) + state[1, g, b].astype(F32)
                 if k == 0:
@@ -423,7 +437,7 @@
         for k in (*FAR_Y, 0):
             g = ys[k]
 
-            @pl.loop(0, NZ)
+            @pl.loop(0, NZ, unroll=True)
             def _(b, g=g, k=k):
                 start = plane_start[g, rows, :] * start_plane[b].astype(F32) + plane_prefix[g, b]
                 if k == 0:
@@ -463,7 +477,7 @@
 
         @pl.loop(0, NY)
         def _(g):
-            @pl.loop(0, NZ)
+            @pl.loop(0, NZ, unroll=True)
             def _(b):
                 before = start_chip[g, b].astype(F32)
                 after = start_factor[g, rows, :] * before + state[0, g, b].astype(F32)
@@ -506,7 +520,7 @@
 
     for copy in table_copies:
         copy.wait_recv()
-    loads[3].wait()
+    loads[2].wait()
     for copy in last_copies:
         copy.wait_recv()
     pooled = [
@@ -607,7 +621,7 @@
         pltpu.VMEM((8, L), F32),
         pltpu.VMEM((NY * NC, 8, L), F32),
         *[ref for _, count in CHUNKS for ref in chunk(count)],
-        dma((4,)), dma((NCH * NY,)),
+        dma((3 + NCH * NY,)), dma((NCH * NY,)),
         dma((2 * NCH,)), dma((2 * NCH,)), dma((NCH, 7)), dma((NCH, 7)),
         dma((NCH, NZ)), dma((NCH, NZ)), dma((NCH, NZ)), dma((NCH, NZ)),
         dma((NZ,)), dma((NZ,)), dma((NX,)), dma((NX,)), dma((32,)), dma((32,)),

time: 43.5 us -> 42.5 us (0.977)
  Pallas kernels: 42.7 us -> 41.7 us
    pallas_call x1, Pallas kernels: 40.7 us -> 39.6 us  [local(): pl.pallas_call(kernel, out_shape=(jax.ShapeDtypeStruct((positions, channe...]
where the time goes in v7:
time: 42.5 us; the launch traced here: 42.3 us
  Pallas kernels  41.7 us (98%)
  between operations  0.64 us (2%)
    pallas_call x1, Pallas kernels, local(): pl.pallas_call(kernel, out_shape=(jax.ShapeDtypeStruct((positions, channe...  39.6 us
    pallas_call x1, Pallas kernels, local(): pl.pallas_call(hand_over, out_shape=(jax.ShapeDtypeStruct(mixed.shape, mi...  2.06 us

profile of v7, /device:TPU:39, one launch (start us, length us, event | category | flops | bytes accessed | tf_op | source)
XLA Modules:
  0.0 42.3 jit_solution(5612059284029157738)
XLA Ops:
  0.6 39.6 %shard_map.68 = (bf16[128,3584]{1,0:T(8,128)(2,1)}, f32[1,128]{1,0:T(1,128)}) custom-call(bf16[128,3584]{1,0:T(8,128)(2,1)} %bitcast.4, bf16[128,256]{1,0:T(8,128)(2,1)} %bitcast.5, f32[56,128]{1,0:T(8,128)} %bitcast.6, f32[56]{0:T(128)} %skip_ref.1, bf16[896,128]{1,0:T(8,128)(2,1)} %cls_ref.1), custom_call_target="tpu_custom_call" | custom-call | tf_op jit(solution)/shard_map/pallas_call | solution.py:629
  40.2 2.1 %shard_map.69 = (bf16[128,3584]{1,0:T(8,128)(2,1)}, f32[1,128]{1,0:T(1,128)}) custom-call(bf16[128,3584]{1,0:T(8,128)(2,1)} %get-tuple-element.6.mixed_in, f32[1,128]{1,0:T(1,128)} %get-tuple-element.7.logits_in), custom_call_target="tpu_custom_call" | custom-call | tf_op jit(solution)/shard_map/pallas_call | solution.py:648

commit v8 on v7

--- a/solution.py
+++ b/solution.py
@@ -20,6 +20,7 @@
 NCH = len(CHUNKS)
 EPS = 1e-06
 PIECES = 8
+EARLY = NZ // 2
 FAR_Y = (2, 1, 3)
 FAR_Z = (4, 5, 3, 6, 2, 7, 1)
 
@@ -60,9 +61,23 @@
     to_x = [{"fsdp": lax.rem(x + k, NX)} for k in range(NX)]
 
     barrier = pltpu.get_barrier_semaphore()
-    partners = to_z[1:] + to_y[1:] + to_y_other[1:] + to_x[1:] + [to_pair]
+    partners = to_y[1:] + to_y_other[1:] + to_x[1:] + [to_pair]
     for who in partners:
         pl.semaphore_signal(barrier, inc=1, device_id=who, device_id_type=MESH)
+    early = z < EARLY
+
+    def greet_along_z(alike):
+        for q in range(NZ):
+            kind = early if q < EARLY else z >= EARLY
+            chosen = kind & (z != q) if alike else jnp.logical_not(kind)
+
+            @pl.when(chosen)
+            def _(q=q):
+                pl.semaphore_signal(
+                    barrier, inc=1, device_id=at(q, y, c), device_id_type=MESH
+                )
+
+    greet_along_z(True)
 
     loads = [
         pltpu.make_async_copy(src, dst, in_s.at[i])
@@ -186,7 +201,9 @@
     for g in range(NY):
         pool_own[g, M:8, :] = jnp.zeros((8 - M, L), F32)
     state_of(0)
-    pl.semaphore_wait(barrier, len(partners))
+    met = len(partners) + EARLY - 1
+    pl.semaphore_wait(barrier, jnp.where(early, met, met + EARLY))
+    greet_along_z(False)
     pair_decay = push(decay_own, decay_pair, small_s.at[0], small_r.at[0], to_pair)
     pair_copies = [send_half(0)]
     for i in range(1, NCH):
@@ -198,9 +215,6 @@
     )
     response[1] = jnp.broadcast_to(jnp.sum(log_decay, axis=1, keepdims=True), (HEADS, L))
     pair_response = push(response, response_pair, small_s.at[1], small_r.at[1], to_pair)
-    table_copies = [
-        push(cls_ref, table.at[x], table_s.at[k], table_r.at[k], to_x[k]) for k in range(1, NX)
-    ]
     cum = lax.dot_general(
         decay_parts, lower, (((1,), (1,)), ((), ())), preferred_element_type=F32
     )
@@ -270,8 +284,16 @@
     axis_note[8:24, :] = summed
     axis_notes[z, 0:8, :] = run
     axis_notes[z, 8:24, :] = summed
+
+    @pl.when(early)
+    def _():
+        pl.semaphore_wait(barrier, NZ - EARLY)
+
     for k in FAR_Z:
         push(axis_note, axis_notes.at[z], note_s.at[k], note_r.at[z], to_z[k])
+    table_copies = [
+        push(cls_ref, table.at[x], table_s.at[k], table_r.at[k], to_x[k]) for k in range(1, NX)
+    ]
     inside(2)
     inside(3)
     mine_1 = jnp.where(c == 0, resp_1, pltpu.roll(resp_1, 64, 1))
@@ -361,6 +383,29 @@
                 for i in range(NCH):
                     buffers[i][7][q] = buffers[i][6][q]
 
+        if q == EARLY:
+            for copy in part_copies:
+                copy.wait_recv()
+            my_half = [
+                jnp.where(c == 0, plane_response[q, 0], pltpu.roll(plane_response[q, 0], 64, 1))[0 : 2 * M, 0:64]
+                for q in range(1, NY)
+            ]
+            pool_rest = (pool_parts[0] + pool_parts[1]) + (pool_parts[2] + pool_parts[3])
+            pool_tiles = []
+            for i, (first, count) in enumerate(CHUNKS):
+                plane_prefix = buffers[i][3]
+                pool_tiles.append(
+                    pool_rows(
+                        my_half,
+                        lambda m, plane_prefix=plane_prefix: [
+                            plane_prefix[q, b, m * 8 : m * 8 + 8, :].astype(BF16)
+                            for q in range(1, NY)
+                            for b in range(NZ)
+                        ],
+                        first, count,
+                    )
+                )
+
         @pl.when(z != q)
         def _(q=q):
             for copy in from_z(q):
@@ -377,27 +422,6 @@
         for i in range(NCH):
             buffers[i][7][...] = jnp.zeros_like(buffers[i][7])
 
-    for copy in part_copies:
-        copy.wait_recv()
-    my_half = [
-        jnp.where(c == 0, plane_response[q, 0], pltpu.roll(plane_response[q, 0], 64, 1))[0 : 2 * M, 0:64]
-        for q in range(1, NY)
-    ]
-    pool_rest = (pool_parts[0] + pool_parts[1]) + (pool_parts[2] + pool_parts[3])
-    pool_tiles = []
-    for i, (first, count) in enumerate(CHUNKS):
-        plane_prefix = buffers[i][3]
-        pool_tiles.append(
-            pool_rows(
-                my_half,
-                lambda m, plane_prefix=plane_prefix: [
-                    plane_prefix[q, b, m * 8 : m * 8 + 8, :].astype(BF16)
-                    for q in range(1, NY)
-                    for b in range(NZ)
-                ],
-                first, count,
-            )
-        )
     lane = lax.broadcasted_iota(jnp.int32, (16, L), 1) // 8
     my_rows = jnp.zeros((16, L), F32)
     for q in range(NZ):

time: 42.5 us -> 42 us (0.988)
  Pallas kernels: 41.7 us -> 40.9 us
    pallas_call x1, Pallas kernels: 39.6 us -> 38.9 us  [local(): pl.pallas_call(kernel, out_shape=(jax.ShapeDtypeStruct((positions, channe...]
where the time goes in v8:
time: 42 us; the launch traced here: 41.6 us
  Pallas kernels  40.9 us (97%)
  between operations  0.64 us (2%)
    pallas_call x1, Pallas kernels, local(): pl.pallas_call(kernel, out_shape=(jax.ShapeDtypeStruct((positions, channe...  38.9 us
    pallas_call x1, Pallas kernels, local(): pl.pallas_call(hand_over, out_shape=(jax.ShapeDtypeStruct(mixed.shape, mi...  2.06 us

profile of v8, /device:TPU:39, one launch (start us, length us, event | category | flops | bytes accessed | tf_op | source)
XLA Modules:
  0.0 41.6 jit_solution(16933888591232510463)
XLA Ops:
  0.6 38.9 %shard_map.68 = (bf16[128,3584]{1,0:T(8,128)(2,1)}, f32[1,128]{1,0:T(1,128)}) custom-call(bf16[128,3584]{1,0:T(8,128)(2,1)} %bitcast.4, bf16[128,256]{1,0:T(8,128)(2,1)} %bitcast.5, f32[56,128]{1,0:T(8,128)} %bitcast.6, f32[56]{0:T(128)} %skip_ref.1, bf16[896,128]{1,0:T(8,128)(2,1)} %cls_ref.1), custom_call_target="tpu_custom_call" | custom-call | tf_op jit(solution)/shard_map/pallas_call | solution.py:653
  39.5 2.1 %shard_map.69 = (bf16[128,3584]{1,0:T(8,128)(2,1)}, f32[1,128]{1,0:T(1,128)}) custom-call(bf16[128,3584]{1,0:T(8,128)(2,1)} %get-tuple-element.6.mixed_in, f32[1,128]{1,0:T(1,128)} %get-tuple-element.7.logits_in), custom_call_target="tpu_custom_call" | custom-call | tf_op jit(solution)/shard_map/pallas_call | solution.py:672

commit v9 on v8

--- a/solution.py
+++ b/solution.py
@@ -20,7 +20,7 @@
 NCH = len(CHUNKS)
 EPS = 1e-06
 PIECES = 8
-EARLY = NZ // 2
+EARLY = 3
 FAR_Y = (2, 1, 3)
 FAR_Z = (4, 5, 3, 6, 2, 7, 1)
 
@@ -201,8 +201,8 @@
     for g in range(NY):
         pool_own[g, M:8, :] = jnp.zeros((8 - M, L), F32)
     state_of(0)
-    met = len(partners) + EARLY - 1
-    pl.semaphore_wait(barrier, jnp.where(early, met, met + EARLY))
+    met = len(partners)
+    pl.semaphore_wait(barrier, jnp.where(early, met + EARLY - 1, met + NZ - 1))
     greet_along_z(False)
     pair_decay = push(decay_own, decay_pair, small_s.at[0], small_r.at[0], to_pair)
     pair_copies = [send_half(0)]

time: 42 us -> 41.6 us (level)
  Pallas kernels: 40.9 us -> 40.3 us
    pallas_call x1, Pallas kernels: 38.9 us -> 38.3 us  [local(): pl.pallas_call(kernel, out_shape=(jax.ShapeDtypeStruct((positions, channe...]
where the time goes in v9:
time: 41.6 us; the launch traced here: 41 us
  Pallas kernels  40.3 us (97%)
  between operations  0.64 us (2%)
    pallas_call x1, Pallas kernels, local(): pl.pallas_call(kernel, out_shape=(jax.ShapeDtypeStruct((positions, channe...  38.3 us
    pallas_call x1, Pallas kernels, local(): pl.pallas_call(hand_over, out_shape=(jax.ShapeDtypeStruct(mixed.shape, mi...  2.06 us

profile of v9, /device:TPU:39, one launch (start us, length us, event | category | flops | bytes accessed | tf_op | source)
XLA Modules:
  0.0 41.0 jit_solution(18245552825716604053)
XLA Ops:
  0.6 38.3 %shard_map.68 = (bf16[128,3584]{1,0:T(8,128)(2,1)}, f32[1,128]{1,0:T(1,128)}) custom-call(bf16[128,3584]{1,0:T(8,128)(2,1)} %bitcast.4, bf16[128,256]{1,0:T(8,128)(2,1)} %bitcast.5, f32[56,128]{1,0:T(8,128)} %bitcast.6, f32[56]{0:T(128)} %skip_ref.1, bf16[896,128]{1,0:T(8,128)(2,1)} %cls_ref.1), custom_call_target="tpu_custom_call" | custom-call | tf_op jit(solution)/shard_map/pallas_call | solution.py:653
  38.9 2.1 %shard_map.69 = (bf16[128,3584]{1,0:T(8,128)(2,1)}, f32[1,128]{1,0:T(1,128)}) custom-call(bf16[128,3584]{1,0:T(8,128)(2,1)} %get-tuple-element.6.mixed_in, f32[1,128]{1,0:T(1,128)} %get-tuple-element.7.logits_in), custom_call_target="tpu_custom_call" | custom-call | tf_op jit(solution)/shard_map/pallas_call | solution.py:672

commit v10 on v9

--- a/solution.py
+++ b/solution.py
@@ -477,6 +477,13 @@
     for copy in earlier:
         copy.wait_send()
 
+    for q in range(1, NZ):
+
+        @pl.when(z != q)
+        def _(q=q):
+            for copy in back(q):
+                copy.wait_send()
+
     for copy in pool_copies:
         copy.wait_recv()
     total = pool_axis[0]
@@ -566,12 +573,6 @@
 
     for store in stores:
         store.wait()
-    for q in range(1, NZ):
-
-        @pl.when(z != q)
-        def _(q=q):
-            for copy in back(q):
-                copy.wait_send()
 
     for copy in sends:
         copy.wait_send()

time: 41.6 us -> 41.6 us (level)
  no operation moved by 1% of the time
where the time goes in v10:
time: 41.6 us; the launch traced here: 41 us
  Pallas kernels  40.3 us (97%)
  between operations  0.64 us (2%)
    pallas_call x1, Pallas kernels, local(): pl.pallas_call(kernel, out_shape=(jax.ShapeDtypeStruct((positions, channe...  38.3 us
    pallas_call x1, Pallas kernels, local(): pl.pallas_call(hand_over, out_shape=(jax.ShapeDtypeStruct(mixed.shape, mi...  2.06 us

profile of v10, /device:TPU:39, one launch (start us, length us, event | category | flops | bytes accessed | tf_op | source)
XLA Modules:
  0.0 41.0 jit_solution(5383602004483236676)
XLA Ops:
  0.6 38.3 %shard_map.68 = (bf16[128,3584]{1,0:T(8,128)(2,1)}, f32[1,128]{1,0:T(1,128)}) custom-call(bf16[128,3584]{1,0:T(8,128)(2,1)} %bitcast.4, bf16[128,256]{1,0:T(8,128)(2,1)} %bitcast.5, f32[56,128]{1,0:T(8,128)} %bitcast.6, f32[56]{0:T(128)} %skip_ref.1, bf16[896,128]{1,0:T(8,128)(2,1)} %cls_ref.1), custom_call_target="tpu_custom_call" | custom-call | tf_op jit(solution)/shard_map/pallas_call | solution.py:654
  38.9 2.1 %shard_map.69 = (bf16[128,3584]{1,0:T(8,128)(2,1)}, f32[1,128]{1,0:T(1,128)}) custom-call(bf16[128,3584]{1,0:T(8,128)(2,1)} %get-tuple-element.6.mixed_in, f32[1,128]{1,0:T(1,128)} %get-tuple-element.7.logits_in), custom_call_target="tpu_custom_call" | custom-call | tf_op jit(solution)/shard_map/pallas_call | solution.py:673
